TPU v7x, 32 devices: a whole 2x2x4 slice. The times are simulated.
32 devices in a mesh: member: 4 (over x, core), tile: 8 (over z, y).
Axes of the slice: x: 2, y: 2, z: 4, core: 2. Of those that a mesh axis runs over, the one named last changes fastest.
Arguments:
- state: bfloat16 [4, 8, 32, 32, 384], P('member', 'tile'), may hold values from -6 to 6
- cotangent: bfloat16 [4, 8, 32, 32, 384], P('member', 'tile'), may hold values from -6 to 6
- neighbors: int32 [8, 8], replicated, may hold values from -1 to 7, as said below
- kernel: float32 [7, 7, 384], replicated, may hold values from -0.875 to 0.875
- conv_bias: float32 [384], replicated, may hold values from -3 to 3
- norm_gain: float32 [384], replicated, may hold values from 0.25 to 1.75
- norm_shift: float32 [384], replicated, may hold values from -2 to 2
- w_in: bfloat16 [384, 1536], replicated, may hold values from -0.3125 to 0.3125
- bias_in: float32 [1536], replicated, may hold values from -3 to 3
- w_out: bfloat16 [1536, 384], replicated, may hold values from -0.15625 to 0.15625
- bias_out: float32 [384], replicated, may hold values from -3 to 3
- layer_scale: float32 [384], replicated, may hold values from 0.3 to 1
Outputs:
- new_state: bfloat16 [4, 8, 32, 32, 384], P('member', 'tile')
- state_grad: bfloat16 [4, 8, 32, 32, 384], P('member', 'tile')
- grad_w_in: float32 [384, 1536], P(None, 'tile')
- grad_w_out: float32 [1536, 384], P('tile')
- grad_kernel: float32 [7, 7, 384], replicated
- grad_bias_in: float32 [1536], replicated
- grad_channels: float32 [5, 384], replicated
Inputs may be any that keep to these rules, and one draw needn't show every extreme that they name: Land tiles and tiles beyond the band's northern or southern edge are -1; longitude wraps around over 6 columns. If neighbors[t, d] = s then neighbors[s, opposite of d] = t. Wet tiles are numbered column by column, the columns of 2 tiles taken alternately upward and downward, so two neighbouring wet tiles differ in index by at most 3, counted cyclically over all wet tiles.
All inputs are finite; a program needn't handle non-finite values.
Results may differ from a plain program's by a relative error of at most 0.0062.
Values may be sent and summed in bfloat16 or wider, within the bound.
A program may use at most 128 MiB of HBM per device.

v0:
```python
import math

import jax
import jax.numpy as jnp
from jax import lax
from jax.sharding import PartitionSpec as P

REACH = 3


GELU_SCALE = 0.7978845608028654
GELU_CUBIC = 0.044715
EPSILON = 1e-06


def shifted(value, axis, steps):
    count = lax.axis_size(axis)
    pairs = [(source, (source + steps) % count) for source in range(count)]
    return lax.ppermute(value, axis, pairs)


def contract_rows(left, right):
    return lax.dot_general(
        left, right, (((0,), (0,)), ((), ())), preferred_element_type=jnp.float32
    )


def contract_cols(left, right):
    return lax.dot_general(
        left, right, (((1,), (1,)), ((), ())), preferred_element_type=jnp.float32
    )


def framed(center, north, south, east, west, north_east, north_west, south_east, south_west):
    lower = jnp.concatenate([south_west, south, south_east], axis=1)
    middle = jnp.concatenate([west, center, east], axis=1)
    upper = jnp.concatenate([north_west, north, north_east], axis=1)
    return jnp.concatenate([lower, middle, upper], axis=0)


def strips(tile, margin):
    edge = tile.shape[0] - margin
    return (tile[:margin], tile[edge:], tile[:, :margin], tile[:, edge:])


def rim_of(tile, margin):
    width = tile.shape[2]
    return jnp.concatenate([piece.reshape(-1, width) for piece in strips(tile, margin)], axis=0)


def keep(pieces, links, source, fresh):
    match = (links == source) & (links >= 0)
    return [jnp.where(match[way], fresh[way], pieces[way]) for way in range(8)]


def from_rim(pieces, links, source, rim, side, margin):
    width = rim.shape[1]
    length = margin * side
    edge = side - margin
    low_rows = rim[:length].reshape(margin, side, width)
    high_rows = rim[length : 2 * length].reshape(margin, side, width)
    low_cols = rim[2 * length : 3 * length].reshape(side, margin, width)
    high_cols = rim[3 * length :].reshape(side, margin, width)
    fresh = [
        low_rows,
        high_rows,
        low_cols,
        high_cols,
        low_rows[:, :margin],
        low_rows[:, edge:],
        high_rows[:, :margin],
        high_rows[:, edge:],
    ]
    return keep(pieces, links, source, fresh)


def assemble(tile, links, myself, count, margin, which):
    side, width = (tile.shape[0], tile.shape[2])
    offsets = list(range(1, REACH + 1)) + [-step for step in range(1, REACH + 1)]
    rows = jnp.zeros((margin, side, width), tile.dtype)
    cols = jnp.zeros((side, margin, width), tile.dtype)
    tip = jnp.zeros((margin, margin, width), tile.dtype)
    pieces = [rows, rows, cols, cols, tip, tip, tip, tip]
    rim = rim_of(tile, margin)
    for offset in offsets:
        source = (myself - offset) % count
        if which == "state":
            moved = shifted(rim, "tile", offset)
        else:
            moved = shifted(rim, "tile", offset)
        pieces = from_rim(pieces, links, source, moved, side, margin)
    return framed(tile, *pieces)


def depthwise(padded, kernel):
    taps = kernel.shape[0]
    side = padded.shape[0] - taps + 1
    total = jnp.zeros((side, side, padded.shape[2]), jnp.float32)
    for row_off in range(taps):
        for col_off in range(taps):
            total = total + kernel[row_off, col_off] * padded[
                row_off : row_off + side, col_off : col_off + side
            ].astype(jnp.float32)
    return total


def transposed(padded, kernel):
    taps = kernel.shape[0]
    side = padded.shape[0] - taps + 1
    total = jnp.zeros((side, side, padded.shape[2]), jnp.float32)
    for row_off in range(taps):
        for col_off in range(taps):
            row_at = taps - 1 - row_off
            col_at = taps - 1 - col_off
            total = total + kernel[row_off, col_off] * padded[
                row_at : row_at + side, col_at : col_at + side
            ].astype(jnp.float32)
    return total


def kernel_grad(padded, grad_mixed):
    taps = padded.shape[0] - grad_mixed.shape[0] + 1
    side = grad_mixed.shape[0]
    rows = []
    for row_off in range(taps):
        line = []
        for col_off in range(taps):
            window = padded[row_off : row_off + side, col_off : col_off + side].astype(jnp.float32)
            line.append(jnp.sum(window * grad_mixed, axis=(0, 1)))
        rows.append(jnp.stack(line))
    return jnp.stack(rows)


def body(
    state,
    cotangent,
    neighbors,
    kernel,
    conv_bias,
    norm_gain,
    norm_shift,
    w_in,
    bias_in,
    w_out,
    bias_out,
    layer_scale,
):
    center = state[0, 0]
    cot_tile = cotangent[0, 0]
    side, width = (center.shape[0], center.shape[2])
    hidden = w_in.shape[1]
    margin = kernel.shape[0] // 2
    count = lax.axis_size("tile")
    myself = lax.axis_index("tile")
    links = neighbors[myself]
    padded = assemble(center, links, myself, count, margin, "state")
    mixed = (depthwise(padded, kernel) + conv_bias).reshape(side * side, width)
    centered = mixed - jnp.mean(mixed, axis=1, keepdims=True)
    variance = jnp.mean(centered * centered, axis=1, keepdims=True)
    inv_std = lax.rsqrt(variance + EPSILON)
    norm_hat = centered * inv_std
    normed = (norm_hat * norm_gain + norm_shift).astype(jnp.bfloat16)
    pre_act = jnp.dot(normed, w_in, preferred_element_type=jnp.float32) + bias_in
    tanh_value = jnp.tanh(GELU_SCALE * (pre_act + GELU_CUBIC * pre_act * pre_act * pre_act))
    activation = (0.5 * pre_act * (1.0 + tanh_value)).astype(jnp.bfloat16)
    branch = jnp.dot(activation, w_out, preferred_element_type=jnp.float32) + bias_out
    flat_state = center.reshape(side * side, width).astype(jnp.float32)
    new_tile = (flat_state + layer_scale * branch).astype(jnp.bfloat16)
    flat_cot = cot_tile.reshape(side * side, width).astype(jnp.float32)
    grad_branch = layer_scale * flat_cot
    branch_low = grad_branch.astype(jnp.bfloat16)
    grad_wout = contract_rows(activation, branch_low)
    grad_bout = jnp.sum(grad_branch, axis=0)
    grad_gamma = jnp.sum(flat_cot * branch, axis=0)
    grad_act = contract_cols(branch_low, w_out)
    slope = 0.5 * (1.0 + tanh_value) + 0.5 * pre_act * (
        1.0 - tanh_value * tanh_value
    ) * GELU_SCALE * (1.0 + 3.0 * GELU_CUBIC * pre_act * pre_act)
    grad_pre = grad_act * slope
    grad_pre_b = grad_pre.astype(jnp.bfloat16)
    grad_win = contract_rows(normed, grad_pre_b)
    grad_bin = jnp.sum(grad_pre, axis=0)
    grad_normed = contract_cols(grad_pre_b, w_in)
    grad_gain = jnp.sum(grad_normed * norm_hat, axis=0)
    grad_shift = jnp.sum(grad_normed, axis=0)
    scaled = grad_normed * norm_gain
    grad_mixed = inv_std * (
        scaled
        - jnp.mean(scaled, axis=1, keepdims=True)
        - norm_hat * jnp.mean(scaled * norm_hat, axis=1, keepdims=True)
    )
    grad_mixed = grad_mixed.reshape(side, side, width)
    grad_low = grad_mixed.astype(jnp.bfloat16)
    padded_grad = assemble(grad_low, links, myself, count, margin, "grad")
    state_grad = (cot_tile.astype(jnp.float32) + transposed(padded_grad, kernel)).astype(
        jnp.bfloat16
    )
    grad_kern = kernel_grad(padded, grad_mixed)
    grad_conv = jnp.sum(grad_mixed, axis=(0, 1))
    share = hidden // count
    (
        grad_win,
        grad_bin,
        grad_kern,
        grad_conv,
        grad_gain,
        grad_shift,
        grad_wout,
        grad_bout,
        grad_gamma,
    ) = lax.psum(
        (
            grad_win,
            grad_bin,
            grad_kern,
            grad_conv,
            grad_gain,
            grad_shift,
            grad_wout,
            grad_bout,
            grad_gamma,
        ),
        ("member", "tile"),
    )
    win_share = lax.dynamic_slice_in_dim(grad_win, myself * share, share, 1)
    wout_share = lax.dynamic_slice_in_dim(grad_wout, myself * share, share, 0)
    factor = 1.0 / math.sqrt(lax.axis_size("member") * count * side * side)
    channels = jnp.stack([grad_conv, grad_gain, grad_shift, grad_bout, grad_gamma]) * factor
    return (
        new_tile.reshape(1, 1, side, side, width),
        state_grad.reshape(1, 1, side, side, width),
        win_share * factor,
        wout_share * factor,
        grad_kern * factor,
        grad_bin * factor,
        channels,
    )


def solution(mesh):
    in_specs = (
        P("member", "tile", None, None, None),
        P("member", "tile", None, None, None),
        P(),
        P(),
        P(),
        P(),
        P(),
        P(),
        P(),
        P(),
        P(),
        P(),
    )
    out_specs = (
        P("member", "tile", None, None, None),
        P("member", "tile", None, None, None),
        P(None, "tile"),
        P("tile", None),
        P(),
        P(),
        P(),
    )
    return jax.shard_map(body, mesh=mesh, in_specs=in_specs, out_specs=out_specs, check_vma=False)
```

profile of v0, /device:TPU:0, one launch (start us, length us, event | category | flops | bytes accessed | tf_op | source)
XLA Modules:
  0.0 402.6 jit_solution(3308788683173243109)
XLA Ops:
  9.6 5.0 %collective-permute-start = (bf16[384,384]{1,0:T(8,128)(2,1)S(1)}, bf16[384,384]{1,0:T(8,128)(2,1)S(1)}, u32[]{:S(2)}, u32[]{:S(2)}) collective-permute-start(bf16[384,384]{1,0:T(8,128)(2,1)S(1)} %pad_maximum_fusion.4), channel_id=1, source_target_pairs={{0,5},{1,6},{2,7},{3,0},{4,1},{5,2},{6,3},{7,4},{8,13},{9,14},{10,... | collective-permute-start | bytes 884744 | tf_op jit(solution)/shard_map/ppermute | solution.py:19
  16.5 1.6 collective-permute-start.3
  18.1 1.6 collective-permute-start.4
  22.6 1.6 slice_reduce_fusion.46
  24.4 6.2 %collective-permute-start.5 = (bf16[384,384]{1,0:T(8,128)(2,1)S(1)}, bf16[384,384]{1,0:T(8,128)(2,1)S(1)}, u32[]{:S(2)}, u32[]{:S(2)}) collective-permute-start(bf16[384,384]{1,0:T(8,128)(2,1)S(1)} %pad_maximum_fusion.4), channel_id=1, source_target_pairs={{0,1},{1,2},{2,3},{3,4},{4,5},{5,6},{6,7},{7,0},{8,9},{9,10},{10,1... | collective-permute-start | bytes 884744 | tf_op jit(solution)/shard_map/ppermute | solution.py:19
  31.9 1.9 slice_reduce_fusion.48
  33.7 1.9 slice_reduce_fusion.47
  35.6 17.9 %collective-permute-done.3 = bf16[384,384]{1,0:T(8,128)(2,1)} collective-permute-done((bf16[384,384]{1,0:T(8,128)(2,1)S(1)}, bf16[384,384]{1,0:T(8,128)(2,1)}, u32[]{:S(2)}, u32[]{:S(2)}) %collective-permute-start.3) | collective-permute-done | bytes 294944 | tf_op jit(solution)/shard_map/ppermute | solution.py:19
  53.5 4.8 %fusion.143 = (bf16[96,384]{1,0:T(8,128)(2,1)S(1)}, bf16[96,384]{1,0:T(8,128)(2,1)S(1)}, bf16[96,384]{1,0:T(8,128)(2,1)S(1)}, bf16[96,384]{1,0:T(8,128)(2,1)S(1)...) fusion(bf16[384,384]{1,0:T(8,128)(2,1)S(1)} %collective-permute-done.5, ...), kind=kLoop, calls=%fused_computation.287 | loop fusion | flops 221184 | bytes 1253382 | tf_op jit(solution)/shard_map/jit(_where)/select_n | solution.py:53
  58.4 4.8 %fusion.193 = (bf16[96,384]{1,0:T(8,128)(2,1)S(1)}, bf16[96,384]{1,0:T(8,128)(2,1)S(1)}, bf16[96,384]{1,0:T(8,128)(2,1)S(1)}, bf16[96,384]{1,0:T(8,128)(2,1)S(1)...) fusion(bf16[384,384]{1,0:T(8,128)(2,1)S(1)} %collective-permute, ...), kind=kLoop, calls=%fused_computation.419 | loop fusion | flops 221184 | bytes 1548294 | tf_op jit(solution)/shard_map/slice | solution.py:61
  63.2 3.7 fusion.173
  67.0 3.6 select_select_fusion.2
  70.6 3.9 fusion.168
  74.5 4.0 fusion.183
  78.5 3.7 select_select_fusion.3
  82.2 3.7 fusion.178
  86.3 4.5 %maximum_maximum_fusion = (bf16[35,38,384]{2,1,0:T(8,128)(2,1)S(1)}, bf16[35,38,384]{2,1,0:T(8,128)(2,1)S(1)}) fusion(bf16[32,3,384]{2,1,0:T(4,128)(2,1)S(1)} %reshape.433, bf16[32,32,384]{2,1,0:T(8,128)(2,1)} %bitcast.189, bf16[32,3,384]{2,1,0:T(4,128)(2,1)S(1)} %reshape.431, bf16[3,3,384]{2,1,0:T(4,128)(2,1)S(1)} %fusion.178, ...), kind=kLoop, calls=%fused_computation.235 | loop fusion | flops 12257280 | bytes 3151872 | tf_op jit(solution)/shard_map/concatenate | solution.py:38
  91.3 13.3 %fusion.185 = (f32[32,32]{1,0:T(8,128)S(1)}, f32[32,32,384]{2,1,0:T(8,128)}) fusion(f32[384]{0:T(512)} %param.16, bf16[35,38,384]{2,1,0:T(8,128)(2,1)S(1)} %get-tuple-element.141, f32[384]{0:T(512)S(1)} %copy-done.26, f32[384]{0:T(512)S(1)} %copy-done.28, f32[384]{0:T(512)S(1)} %copy-done.32, f32[384]{0:T(512)S(1)} %copy-done.34, f32[384]{0:T(512)S(1)} %copy-done.36, ...), kind=kLoop, calls=%fused_computation.412 | loop fusion | flops 65272832 | bytes 35617792 | tf_op jit(solution)/shard_map/reduce_sum | solution.py:158
  104.7 1.8 multiply_reduce_fusion.2
  106.6 1.8 add_convert_fusion
  108.4 2.9 multiply_convert_fusion
  111.4 3.5 fusion.108
  114.9 6.3 %fusion.200 = (f32[1536]{0:T(1024)}, bf16[1024,1536]{1,0:T(8,128)(2,1)S(1)}) fusion(f32[1024,1536]{1,0:T(8,128)S(1)} %get-tuple-element.233, f32[1536]{0:T(1024)S(1)} %copy-done.109, bf16[1024,384]{1,0:T(8,128)(2,1)S(1)} %get-tuple-element.142, bf16[1536,384]{1,0:T(8,128)(2,1)S(1)} %copy-done.108), kind=kOutput, calls=%fused_computation.426 | convolution fusion | flops 1240988160 | bytes 11415552 | tf_op jit(solution)/shard_map/dot_general | solution.py:29
  121.2 2.7 multiply_reduce_fusion
  123.8 5.8 %fusion.101 = (f32[384]{0:T(512)S(1)}, f32[384]{0:T(512)}, f32[384]{0:T(512)}, f32[384]{0:T(512)}, f32[384]{0:T(512)}, /*index=5*/f32[384]{0:T(512)}, f32[384]{0...) fusion(bf16[35,38,384]{2,1,0:T(8,128)(2,1)S(1)} %get-tuple-elem, ...), kind=kLoop, calls=%fused_computation.202 | loop fusion | flops 23979264 | bytes 18919936 | tf_op jit(solution)/shard_map/reduce_sum | solution.py:129
  130.6 3.6 fusion.83
  134.3 4.4 %fusion.51 = (f32[384]{0:T(512)S(1)}, f32[384]{0:T(512)}, f32[384]{0:T(512)}, f32[384]{0:T(512)}, f32[384]{0:T(512)}, /*index=5*/f32[384]{0:T(512)}, f32[384]{0:...) fusion(bf16[35,38,384]{2,1,0:T(8,128)(2,1)S(1)} %get-tuple-elem, ...), kind=kLoop, calls=%fused_computation.152 | loop fusion | flops 21226752 | bytes 15756288 | tf_op jit(solution)/shard_map/reduce_sum | solution.py:129
  138.7 3.2 fusion.201
  141.9 3.3 fusion.110
  146.2 2.1 collective-permute-start.11
  148.3 2.7 collective-permute-start.6
  151.0 2.1 collective-permute-start.7
  199.3 39.4 %all-reduce = (f32[1536]{0:T(1024)S(1)}, f32[1,384]{1,0:T(1,128)S(1)}, f32[1,384]{1,0:T(1,128)S(1)}, f32[1,384]{1,0:T(1,128)}, f32[1,384]{1,0:T(1,128)}, /*index=5*/f32[1,384]{1,0:T(1,128)}) all-reduce(f32[1536]{0:T(1024)} %get-tuple-element.235, f32[1,384]{1,0:T(1,128)} %stack.274, ...), channel_id=1, replica_groups=mesh['member'=4,'tile'=8] {'member','tile'}, use_global_device_ids=true, to_apply=%region_57.58 | all-reduce | flops 3456 | bytes 27648 | tf_op jit(solution)/shard_map/psum | solution.py:211
  238.7 4.1 %collective-permute-start.9 = (bf16[384,384]{1,0:T(8,128)(2,1)S(1)}, bf16[384,384]{1,0:T(8,128)(2,1)}, u32[]{:S(2)}, u32[]{:S(2)}) collective-permute-start(bf16[384,384]{1,0:T(8,128)(2,1)S(1)} %pad_maximum_fusion.5), channel_id=1, source_target_pairs={{0,3},{1,4},{2,5},{3,6},{4,7},{5,0},{6,1},{7,2},{8,11},{9,12},{10,... | collective-permute-start | bytes 884744 | tf_op jit(solution)/shard_map/ppermute | solution.py:19
  244.7 15.3 %collective-permute-done.9 = bf16[384,384]{1,0:T(8,128)(2,1)} collective-permute-done((bf16[384,384]{1,0:T(8,128)(2,1)S(1)}, bf16[384,384]{1,0:T(8,128)(2,1)}, u32[]{:S(2)}, u32[]{:S(2)}) %collective-permute-start.9) | collective-permute-done | bytes 294944 | tf_op jit(solution)/shard_map/ppermute | solution.py:19
  260.0 4.8 %fusion.192 = (bf16[96,384]{1,0:T(8,128)(2,1)S(1)}, bf16[96,384]{1,0:T(8,128)(2,1)S(1)}, bf16[96,384]{1,0:T(8,128)(2,1)S(1)}, bf16[96,384]{1,0:T(8,128)(2,1)S(1)...) fusion(bf16[384,384]{1,0:T(8,128)(2,1)S(1)} %collective-permute-done.7, ...), kind=kLoop, calls=%fused_computation.418 | loop fusion | flops 221184 | bytes 1253382 | tf_op jit(solution)/shard_map/slice | solution.py:61
  264.8 4.9 %fusion.191 = (bf16[96,384]{1,0:T(8,128)(2,1)S(1)}, bf16[96,384]{1,0:T(8,128)(2,1)S(1)}, bf16[96,384]{1,0:T(8,128)(2,1)S(1)}, bf16[96,384]{1,0:T(8,128)(2,1)S(1)...) fusion(bf16[384,384]{1,0:T(8,128)(2,1)S(1)} %collective-permute, ...), kind=kLoop, calls=%fused_computation.417 | loop fusion | flops 221184 | bytes 1548294 | tf_op jit(solution)/shard_map/slice | solution.py:60
  269.6 4.0 fusion.153
  273.6 3.7 select_select_fusion
  277.3 3.7 fusion.148
  281.0 3.7 fusion.163
  284.7 3.6 select_select_fusion.1
  288.4 3.9 fusion.158
  292.8 3.5 maximum_maximum_fusion.2
  296.7 13.8 %fusion.123 = bf16[1,1,32,32,384]{4,3,2,1,0:T(8,128)(2,1)} fusion(bf16[35,38,384]{2,1,0:T(8,128)(2,1)S(1)} %get-tuple-element.139, f32[384]{0:T(512)S(1)} %copy-done.27, f32[384]{0:T(512)S(1)} %copy-done.29, f32[384]{0:T(512)S(1)} %copy-done.33, f32[384]{0:T(512)S(1)} %copy-done.35, f32[384]{0:T(512)S(1)} %copy-done.37, f32[384]{0:T(512)S(1)} %copy-done.39, ...), kind=kLoop, calls=%fused_computation.259 | loop fusion | flops 65667072 | bytes 35612160 | tf_op jit(solution)/shard_map/reshape | solution.py:231
  310.5 80.3 %all-reduce.4.cloned.1.call-done = (f32[384,1536]{0,1:T(8,128)}, f32[1536,384]{1,0:T(8,128)}, f32[7,7,384]{2,1,0:T(8,128)}) async-done(((f32[384,1536]{0,1:T(8,128)}, f32[1536,384]{1,0:T(8,128)}, f32[7,7,384]{2,1,0:T(8,128)}), (f32[384,1536]{0,1:T(8,128)}, f32[1536,384]{1,0:T(8,128)}, f32[7,7,384]{2,1,0:T(8,128)})) %all-reduce.4.cloned.1.call-update) | async-done | bytes 4793872 | tf_op jit(solution)/shard_map/psum | solution.py:211
  390.8 1.7 dynamic-slice_multiply_fusion
  392.5 1.7 dynamic-slice_multiply_fusion.1
  (339 shorter events, 60.8 us)
Async XLA Ops:
  7.2 101.2 %copy-start = (bf16[384,1536]{1,0:T(8,128)(2,1)S(1)}, bf16[384,1536]{1,0:T(8,128)(2,1)}, u32[]{:S(2)}) copy-start(bf16[384,1536]{1,0:T(8,128)(2,1)} %param.19) | copy-start | bytes 3538948
  7.2 17.0 %copy-start.4 = (bf16[1,1,32,32,384]{4,3,2,1,0:T(8,128)(2,1)S(1)}, bf16[1,1,32,32,384]{4,3,2,1,0:T(8,128)(2,1)}, u32[]{:S(2)}) copy-start(bf16[1,1,32,32,384]{4,3,2,1,0:T(8,128)(2,1)} %param.13) | copy-start | bytes 2359300
  7.2 17.0 %copy-start.103 = (f32[384]{0:T(512)S(1)}, f32[384]{0:T(512)}, u32[]{:S(2)}) copy-start(f32[384]{0:T(512)} %param.23) | copy-start | bytes 4612
  7.2 383.6 %all-reduce.4.cloned.1.call-start = ((), (), s32[]{:S(2)}) async-start(), calls=%async_computation | async-start | bytes 9609216 | tf_op jit(solution)/shard_map/psum | solution.py:211
  9.6 14.8 %collective-permute-start = (bf16[384,384]{1,0:T(8,128)(2,1)S(1)}, bf16[384,384]{1,0:T(8,128)(2,1)S(1)}, u32[]{:S(2)}, u32[]{:S(2)}) collective-permute-start(bf16[384,384]{1,0:T(8,128)(2,1)S(1)} %pad_maximum_fusion.4), channel_id=1, source_target_pairs={{0,5},{1,6},{2,7},{3,0},{4,1},{5,2},{6,3},{7,4},{8,13},{9,14},{10,... | collective-permute-start | bytes 884744 | tf_op jit(solution)/shard_map/ppermute | solution.py:19
  14.7 21.0 %collective-permute-start.1 = (bf16[384,384]{1,0:T(8,128)(2,1)S(1)}, bf16[384,384]{1,0:T(8,128)(2,1)S(1)}, u32[]{:S(2)}, u32[]{:S(2)}) collective-permute-start(bf16[384,384]{1,0:T(8,128)(2,1)S(1)} %pad_maximum_fusion.4), channel_id=1, source_target_pairs={{0,6},{1,7},{2,0},{3,1},{4,2},{5,3},{6,4},{7,5},{8,14},{9,15},{10,... | collective-permute-start | bytes 884744 | tf_op jit(solution)/shard_map/ppermute | solution.py:19
  16.0 19.6 %collective-permute-start.2 = (bf16[384,384]{1,0:T(8,128)(2,1)S(1)}, bf16[384,384]{1,0:T(8,128)(2,1)S(1)}, u32[]{:S(2)}, u32[]{:S(2)}) collective-permute-start(bf16[384,384]{1,0:T(8,128)(2,1)S(1)} %pad_maximum_fusion.4), channel_id=1, source_target_pairs={{0,7},{1,0},{2,1},{3,2},{4,3},{5,4},{6,5},{7,6},{8,15},{9,8},{10,9... | collective-permute-start | bytes 884744 | tf_op jit(solution)/shard_map/ppermute | solution.py:19
  16.5 37.0 %collective-permute-start.3 = (bf16[384,384]{1,0:T(8,128)(2,1)S(1)}, bf16[384,384]{1,0:T(8,128)(2,1)}, u32[]{:S(2)}, u32[]{:S(2)}) collective-permute-start(bf16[384,384]{1,0:T(8,128)(2,1)S(1)} %pad_maximum_fusion.4), channel_id=1, source_target_pairs={{0,3},{1,4},{2,5},{3,6},{4,7},{5,0},{6,1},{7,2},{8,11},{9,12},{10,... | collective-permute-start | bytes 884744 | tf_op jit(solution)/shard_map/ppermute | solution.py:19
  18.1 35.4 %collective-permute-start.4 = (bf16[384,384]{1,0:T(8,128)(2,1)S(1)}, bf16[384,384]{1,0:T(8,128)(2,1)}, u32[]{:S(2)}, u32[]{:S(2)}) collective-permute-start(bf16[384,384]{1,0:T(8,128)(2,1)S(1)} %pad_maximum_fusion.4), channel_id=1, source_target_pairs={{0,2},{1,3},{2,4},{3,5},{4,6},{5,7},{6,0},{7,1},{8,10},{9,11},{10,... | collective-permute-start | bytes 884744 | tf_op jit(solution)/shard_map/ppermute | solution.py:19
  24.2 66.6 %copy-start.8 = (f32[384]{0:T(512)}, f32[384]{0:T(512)S(1)}, u32[]{:S(2)}) copy-start(f32[384]{0:T(512)S(1)} %get-tuple-element.111) | copy-start | bytes 4612
  24.2 66.7 %copy-start.10 = (f32[384]{0:T(512)}, f32[384]{0:T(512)S(1)}, u32[]{:S(2)}) copy-start(f32[384]{0:T(512)S(1)} %get-tuple-element.112) | copy-start | bytes 4612
  24.2 66.7 %copy-start.12 = (f32[384]{0:T(512)}, f32[384]{0:T(512)S(1)}, u32[]{:S(2)}) copy-start(f32[384]{0:T(512)S(1)} %get-tuple-element.113) | copy-start | bytes 4612
  24.2 66.7 %copy-start.14 = (f32[384]{0:T(512)}, f32[384]{0:T(512)S(1)}, u32[]{:S(2)}) copy-start(f32[384]{0:T(512)S(1)} %get-tuple-element.114) | copy-start | bytes 4612
  24.4 29.1 %collective-permute-start.5 = (bf16[384,384]{1,0:T(8,128)(2,1)S(1)}, bf16[384,384]{1,0:T(8,128)(2,1)S(1)}, u32[]{:S(2)}, u32[]{:S(2)}) collective-permute-start(bf16[384,384]{1,0:T(8,128)(2,1)S(1)} %pad_maximum_fusion.4), channel_id=1, source_target_pairs={{0,1},{1,2},{2,3},{3,4},{4,5},{5,6},{6,7},{7,0},{8,9},{9,10},{10,1... | collective-permute-start | bytes 884744 | tf_op jit(solution)/shard_map/ppermute | solution.py:19
  85.9 5.0 %copy-start.2 = (bf16[1,1,32,32,384]{4,3,2,1,0:T(8,128)(2,1)S(1)}, bf16[1,1,32,32,384]{4,3,2,1,0:T(8,128)(2,1)}, u32[]{:S(2)}) copy-start(bf16[1,1,32,32,384]{4,3,2,1,0:T(8,128)(2,1)} %param.12) | copy-start | bytes 2359300
  85.9 5.0 %copy-start.16 = (f32[384]{0:T(512)S(1)}, f32[384]{0:T(512)}, u32[]{:S(2)}) copy-start(f32[384]{0:T(512)} %get-tuple-element.115) | copy-start | bytes 4612
  85.9 5.0 %copy-start.18 = (f32[384]{0:T(512)S(1)}, f32[384]{0:T(512)}, u32[]{:S(2)}) copy-start(f32[384]{0:T(512)} %get-tuple-element.116) | copy-start | bytes 4612
  85.9 5.0 %copy-start.20 = (f32[384]{0:T(512)S(1)}, f32[384]{0:T(512)}, u32[]{:S(2)}) copy-start(f32[384]{0:T(512)} %get-tuple-element.117) | copy-start | bytes 4612
  85.9 5.0 %copy-start.22 = (f32[384]{0:T(512)S(1)}, f32[384]{0:T(512)}, u32[]{:S(2)}) copy-start(f32[384]{0:T(512)} %get-tuple-element.118) | copy-start | bytes 4612
  85.9 5.0 %copy-start.24 = (f32[384]{0:T(512)S(1)}, f32[384]{0:T(512)}, u32[]{:S(2)}) copy-start(f32[384]{0:T(512)} %get-tuple-element.119) | copy-start | bytes 4612
  86.0 5.0 %copy-start.26 = (f32[384]{0:T(512)S(1)}, f32[384]{0:T(512)}, u32[]{:S(2)}) copy-start(f32[384]{0:T(512)} %get-tuple-element.120) | copy-start | bytes 4612
  86.0 5.0 %copy-start.28 = (f32[384]{0:T(512)S(1)}, f32[384]{0:T(512)}, u32[]{:S(2)}) copy-start(f32[384]{0:T(512)} %get-tuple-element.121) | copy-start | bytes 4612
  86.0 5.0 %copy-start.30 = (f32[384]{0:T(512)S(1)}, f32[384]{0:T(512)}, u32[]{:S(2)}) copy-start(f32[384]{0:T(512)} %get-tuple-element.73) | copy-start | bytes 4612
  86.0 5.0 %copy-start.32 = (f32[384]{0:T(512)S(1)}, f32[384]{0:T(512)}, u32[]{:S(2)}) copy-start(f32[384]{0:T(512)} %get-tuple-element.74) | copy-start | bytes 4612
  86.0 5.0 %copy-start.34 = (f32[384]{0:T(512)S(1)}, f32[384]{0:T(512)}, u32[]{:S(2)}) copy-start(f32[384]{0:T(512)} %get-tuple-element.75) | copy-start | bytes 4612
  86.0 5.0 %copy-start.36 = (f32[384]{0:T(512)S(1)}, f32[384]{0:T(512)}, u32[]{:S(2)}) copy-start(f32[384]{0:T(512)} %get-tuple-element.76) | copy-start | bytes 4612
  86.0 5.0 %copy-start.38 = (f32[384]{0:T(512)S(1)}, f32[384]{0:T(512)}, u32[]{:S(2)}) copy-start(f32[384]{0:T(512)} %get-tuple-element.77) | copy-start | bytes 4612
  114.9 6.3 %copy-start.1 = (f32[32,32,384]{2,1,0:T(8,128)S(1)}, f32[32,32,384]{2,1,0:T(8,128)}, u32[]{:S(2)}) copy-start(f32[32,32,384]{2,1,0:T(8,128)} %get-tuple-element.133) | copy-start | bytes 4718596
  114.9 6.3 %copy-start.89 = (f32[384]{0:T(512)S(1)}, f32[384]{0:T(512)}, u32[]{:S(2)}) copy-start(f32[384]{0:T(512)} %param.17) | copy-start | bytes 4612
  145.1 12.2 %copy-start.102 = (f32[384]{0:T(512)S(1)}, f32[384]{0:T(512)}, u32[]{:S(2)}) copy-start(f32[384]{0:T(512)} %get-tuple-element.19) | copy-start | bytes 4612
  145.1 12.7 %copy-start.101 = (f32[384]{0:T(512)S(1)}, f32[384]{0:T(512)}, u32[]{:S(2)}) copy-start(f32[384]{0:T(512)} %get-tuple-element.18) | copy-start | bytes 4612
  145.1 13.3 %copy-start.100 = (f32[384]{0:T(512)S(1)}, f32[384]{0:T(512)}, u32[]{:S(2)}) copy-start(f32[384]{0:T(512)} %get-tuple-element.17) | copy-start | bytes 4612
  145.1 13.9 %copy-start.99 = (f32[384]{0:T(512)S(1)}, f32[384]{0:T(512)}, u32[]{:S(2)}) copy-start(f32[384]{0:T(512)} %get-tuple-element.16) | copy-start | bytes 4612
  145.2 18.2 %copy-start.98 = (f32[384]{0:T(512)S(1)}, f32[384]{0:T(512)}, u32[]{:S(2)}) copy-start(f32[384]{0:T(512)} %get-tuple-element.26) | copy-start | bytes 4612
  145.2 18.8 %copy-start.97 = (f32[384]{0:T(512)S(1)}, f32[384]{0:T(512)}, u32[]{:S(2)}) copy-start(f32[384]{0:T(512)} %get-tuple-element.25) | copy-start | bytes 4612
  145.2 19.4 %copy-start.95 = (f32[384]{0:T(512)S(1)}, f32[384]{0:T(512)}, u32[]{:S(2)}) copy-start(f32[384]{0:T(512)} %get-tuple-element.24) | copy-start | bytes 4612
  145.2 20.0 %copy-start.94 = (f32[384]{0:T(512)S(1)}, f32[384]{0:T(512)}, u32[]{:S(2)}) copy-start(f32[384]{0:T(512)} %get-tuple-element.23) | copy-start | bytes 4612
  145.2 27.8 %copy-start.96 = (f32[384]{0:T(512)S(1)}, f32[384]{0:T(512)}, u32[]{:S(2)}) copy-start(f32[384]{0:T(512)} %get-tuple-element.63) | copy-start | bytes 4612
  145.2 40.3 %copy-start.93 = (f32[384]{0:T(512)S(1)}, f32[384]{0:T(512)}, u32[]{:S(2)}) copy-start(f32[384]{0:T(512)} %get-tuple-element.64) | copy-start | bytes 4612
  145.3 52.6 %copy-start.92 = (f32[384]{0:T(512)S(1)}, f32[384]{0:T(512)}, u32[]{:S(2)}) copy-start(f32[384]{0:T(512)} %get-tuple-element.12) | copy-start | bytes 4612
  145.3 53.2 %copy-start.91 = (f32[384]{0:T(512)S(1)}, f32[384]{0:T(512)}, u32[]{:S(2)}) copy-start(f32[384]{0:T(512)} %get-tuple-element.11) | copy-start | bytes 4612
  145.3 53.2 %copy-start.90 = (f32[384]{0:T(512)S(1)}, f32[384]{0:T(512)}, u32[]{:S(2)}) copy-start(f32[384]{0:T(512)} %get-tuple-element.10) | copy-start | bytes 4612
  145.6 93.0 %collective-permute-start.10 = (bf16[384,384]{1,0:T(8,128)(2,1)S(1)}, bf16[384,384]{1,0:T(8,128)(2,1)S(1)}, u32[]{:S(2)}, u32[]{:S(2)}) collective-permute-start(bf16[384,384]{1,0:T(8,128)(2,1)S(1)} %pad_maximum_fusion.5), channel_id=1, source_target_pairs={{0,2},{1,3},{2,4},{3,5},{4,6},{5,7},{6,0},{7,1},{8,10},{9,11},{10,... | collective-permute-start | bytes 884744 | tf_op jit(solution)/shard_map/ppermute | solution.py:19
  146.2 98.5 %collective-permute-start.11 = (bf16[384,384]{1,0:T(8,128)(2,1)S(1)}, bf16[384,384]{1,0:T(8,128)(2,1)S(1)}, u32[]{:S(2)}, u32[]{:S(2)}) collective-permute-start(bf16[384,384]{1,0:T(8,128)(2,1)S(1)} %pad_maximum_fusion.5), channel_id=1, source_target_pairs={{0,1},{1,2},{2,3},{3,4},{4,5},{5,6},{6,7},{7,0},{8,9},{9,10},{10,1... | collective-permute-start | bytes 884744 | tf_op jit(solution)/shard_map/ppermute | solution.py:19
  148.3 96.4 %collective-permute-start.6 = (bf16[384,384]{1,0:T(8,128)(2,1)S(1)}, bf16[384,384]{1,0:T(8,128)(2,1)S(1)}, u32[]{:S(2)}, u32[]{:S(2)}) collective-permute-start(bf16[384,384]{1,0:T(8,128)(2,1)S(1)} %pad_maximum_fusion.5), channel_id=1, source_target_pairs={{0,5},{1,6},{2,7},{3,0},{4,1},{5,2},{6,3},{7,4},{8,13},{9,14},{10,... | collective-permute-start | bytes 884744 | tf_op jit(solution)/shard_map/ppermute | solution.py:19
  151.0 93.7 %collective-permute-start.7 = (bf16[384,384]{1,0:T(8,128)(2,1)S(1)}, bf16[384,384]{1,0:T(8,128)(2,1)S(1)}, u32[]{:S(2)}, u32[]{:S(2)}) collective-permute-start(bf16[384,384]{1,0:T(8,128)(2,1)S(1)} %pad_maximum_fusion.5), channel_id=1, source_target_pairs={{0,6},{1,7},{2,0},{3,1},{4,2},{5,3},{6,4},{7,5},{8,14},{9,15},{10,... | collective-permute-start | bytes 884744 | tf_op jit(solution)/shard_map/ppermute | solution.py:19
  153.0 91.7 %collective-permute-start.8 = (bf16[384,384]{1,0:T(8,128)(2,1)S(1)}, bf16[384,384]{1,0:T(8,128)(2,1)}, u32[]{:S(2)}, u32[]{:S(2)}) collective-permute-start(bf16[384,384]{1,0:T(8,128)(2,1)S(1)} %pad_maximum_fusion.5), channel_id=1, source_target_pairs={{0,7},{1,0},{2,1},{3,2},{4,3},{5,4},{6,5},{7,6},{8,15},{9,8},{10,9... | collective-permute-start | bytes 884744 | tf_op jit(solution)/shard_map/ppermute | solution.py:19
  238.7 21.3 %collective-permute-start.9 = (bf16[384,384]{1,0:T(8,128)(2,1)S(1)}, bf16[384,384]{1,0:T(8,128)(2,1)}, u32[]{:S(2)}, u32[]{:S(2)}) collective-permute-start(bf16[384,384]{1,0:T(8,128)(2,1)S(1)} %pad_maximum_fusion.5), channel_id=1, source_target_pairs={{0,3},{1,4},{2,5},{3,6},{4,7},{5,0},{6,1},{7,2},{8,11},{9,12},{10,... | collective-permute-start | bytes 884744 | tf_op jit(solution)/shard_map/ppermute | solution.py:19
  (76 other events, 309.4 us)
Sparse Core Ops, SparseCore 0:
  243.5 147.2 all-reduce.3
where the time goes:
time: 405 us; the launch traced here: 403 us
  other arithmetic  125 us (31%)
  waiting for transfers between devices  113 us (28%)
  local copies, waits for them, and re-layouts  58.3 us (14%)
  blocking collectives  39.4 us (10%)
  starting transfers between devices  28.4 us (7%)
  matrix products  21.8 us (5%)
  between operations  15.9 us (4%)
    psum x1, waiting for transfers between devices, body(): lax.psum((grad_win, grad_bin, grad_kern, grad_conv, grad_gain, grad_shift...  80.3 us
    select_n x13, other arithmetic, keep(): return [jnp.where(match[way], fresh[way], pieces[way]) for way in range(8)]  50 us
    another operation x56, local copies, waits for them, and re-layouts, kernel_grad(): rows.append(jnp.stack(line))  40.6 us
    psum x1, blocking collectives, body(): lax.psum((grad_win, grad_bin, grad_kern, grad_conv, grad_gain, grad_shift...  39.4 us
    ppermute x12, waiting for transfers between devices, shifted(): return lax.ppermute(value, axis, pairs)  33.2 us
    ppermute x12, starting transfers between devices, shifted(): return lax.ppermute(value, axis, pairs)  28.3 us
    reduce_sum x3, other arithmetic, kernel_grad(): line.append(jnp.sum(window * grad_mixed, axis=(0, 1)))  13.9 us
    reshape x1, other arithmetic, body(): state_grad.reshape(1, 1, side, side, width)  13.8 us
  transfers between devices with their start and end apart: 13, of which 3 were waited for; matrix products, arithmetic and copies ran while one was open for 26% of the time, Pallas kernels for 0%

commit v1 on v0

v1 whole, which is shorter than its diff:
```python
import functools
import math

import jax
import jax.numpy as jnp
from jax import lax
from jax.experimental import pallas as pl
from jax.experimental.pallas import tpu as pltpu
from jax.sharding import PartitionSpec as P

OFFSETS = (1, 2, 3, -1, -2, -3)
GELU_SCALE = 0.7978845608028654
GELU_CUBIC = 0.044715
EPSILON = 1e-06
LANES = 128
LEAD = 8
MESH = pl.DeviceIdType.MESH
F32 = jnp.float32
BF16 = jnp.bfloat16
VMEM_LIMIT = 56 << 20


def vmem_spec():
    return pl.BlockSpec(memory_space=pltpu.VMEM)


def smem_spec():
    return pl.BlockSpec(memory_space=pltpu.SMEM)


def local_params():
    return pltpu.CompilerParams(vmem_limit_bytes=VMEM_LIMIT)


def payload_kernel(side, margin, want_ref, tile_ref, out_ref, wide):
    wide[...] = tile_ref[...].astype(F32)
    edge = side - margin
    for slot in range(len(OFFSETS)):
        for way in range(8):

            @pl.when(want_ref[slot, way] == 1)
            def _():
                for k in range(margin):
                    if way == 0:
                        line = wide[pl.ds(k * side, side), :]
                    elif way == 1:
                        line = wide[pl.ds((edge + k) * side, side), :]
                    elif way == 2:
                        line = wide[pl.ds(k, side, stride=side), :]
                    elif way == 3:
                        line = wide[pl.ds(edge + k, side, stride=side), :]
                    else:
                        row = k if way in (4, 5) else edge + k
                        start = 0 if way in (4, 6) else side - 8
                        line = jnp.concatenate(
                            [wide[pl.ds(row * side + start, 8), :]] * (side // 8), axis=0
                        )
                    out_ref[slot, k] = line.astype(BF16)


def payload(want, tile, side, margin):
    width = tile.shape[1]
    return pl.pallas_call(
        functools.partial(payload_kernel, side, margin),
        grid=(width // LANES,),
        in_specs=[smem_spec(), pl.BlockSpec((side * side, LANES), lambda c: (0, c))],
        out_specs=pl.BlockSpec((len(OFFSETS), margin, side, LANES), lambda c: (0, 0, 0, c)),
        out_shape=jax.ShapeDtypeStruct((len(OFFSETS), margin, side, width), BF16),
        scratch_shapes=[pltpu.VMEM((side * side, LANES), F32)],
        compiler_params=local_params(),
        name="payload",
    )(want, tile)


def exchange_kernel(count, send_ref, recv_ref, send_sem, recv_sem):
    me = lax.axis_index("tile")
    barrier = pltpu.get_barrier_semaphore()
    peers = [lax.rem(me + offset + count, count) for offset in OFFSETS]
    for peer in peers:
        pl.semaphore_signal(barrier, inc=1, device_id={"tile": peer}, device_id_type=MESH)
    pl.semaphore_wait(barrier, len(OFFSETS))
    copies = []
    for slot, peer in enumerate(peers):
        copy = pltpu.make_async_remote_copy(
            src_ref=send_ref.at[slot],
            dst_ref=recv_ref.at[slot],
            send_sem=send_sem.at[slot],
            recv_sem=recv_sem.at[slot],
            device_id={"tile": peer},
            device_id_type=MESH,
        )
        copy.start()
        copies.append(copy)
    for copy in copies:
        copy.wait()


def exchange(pieces, count, ident):
    return pl.pallas_call(
        functools.partial(exchange_kernel, count),
        in_specs=[vmem_spec()],
        out_specs=vmem_spec(),
        out_shape=jax.ShapeDtypeStruct(pieces.shape, pieces.dtype),
        scratch_shapes=[
            pltpu.SemaphoreType.DMA((len(OFFSETS),)),
            pltpu.SemaphoreType.DMA((len(OFFSETS),)),
        ],
        compiler_params=pltpu.CompilerParams(
            collective_id=ident, has_side_effects=True, vmem_limit_bytes=VMEM_LIMIT
        ),
        name="exchange",
    )(pieces)


def stride_of(side):
    return side + 2 * LEAD


def fill(padded, side, margin, have_ref, recv_ref):
    pitch = stride_of(side)
    for slot in range(len(OFFSETS)):
        for way in range(8):

            @pl.when(have_ref[slot, way] == 1)
            def _():
                for k in range(margin):
                    line = recv_ref[slot, k].astype(F32)
                    if way == 0:
                        padded[pl.ds((margin + side + k) * pitch + LEAD, side), :] = line
                    elif way == 1:
                        padded[pl.ds(k * pitch + LEAD, side), :] = line
                    elif way == 2:
                        padded[pl.ds(margin * pitch + LEAD + side + k, side, stride=pitch), :] = line
                    elif way == 3:
                        padded[pl.ds(margin * pitch + LEAD - margin + k, side, stride=pitch), :] = line
                    else:
                        row = margin + side + k if way in (4, 5) else k
                        start = LEAD + side if way in (4, 6) else LEAD - 8
                        padded[pl.ds(row * pitch + start, 8), :] = line[:8]


def place(padded, side, margin, center, have_ref, recv_ref):
    pitch = stride_of(side)
    rows = side + 2 * margin
    padded[...] = jnp.zeros_like(padded)
    for row in range(side):
        padded[pl.ds((margin + row) * pitch + LEAD, side), :] = center(row)
    del rows
    fill(padded, side, margin, have_ref, recv_ref)


def convolve(padded, kern_ref, side, taps, flipped, emit, group=4):
    pitch = stride_of(side)
    margin = taps // 2

    def step(index, carry):
        base = index * group
        total = [jnp.zeros((side, LANES), F32) for _ in range(group)]
        for col in range(taps):
            for row in range(group + taps - 1):
                start = (base + row) * pitch
                line = padded[pl.ds(start + (LEAD - margin + col), side), :]
                for out in range(group):
                    up = row - out
                    if 0 <= up < taps:
                        at = (taps - 1 - up) * taps + taps - 1 - col if flipped else up * taps + col
                        total[out] = total[out] + kern_ref[pl.ds(at, 1), :] * line
        for out in range(group):
            emit(base + out, total[out])
        return carry

    lax.fori_loop(0, side // group, step, 0)


def forward_kernel(side, taps, have_ref, tile_ref, recv_ref, kern_ref, bias_ref, mixed_ref, padded):
    margin = taps // 2

    def center(row):
        return tile_ref[pl.ds(row * side, side), :].astype(F32)

    place(padded, side, margin, center, have_ref, recv_ref)

    def emit(row, value):
        mixed_ref[pl.ds(pl.multiple_of(row * side, side), side), :] = value + bias_ref[...]

    convolve(padded, kern_ref, side, taps, False, emit)


def forward_conv(have, tile, recv, kern, bias, side, taps):
    width = tile.shape[1]
    margin = taps // 2
    cells = side * side
    spread = (side + 2 * margin) * stride_of(side)
    lane = lambda c: (0, c)
    return pl.pallas_call(
        functools.partial(forward_kernel, side, taps),
        grid=(width // LANES,),
        in_specs=[
            smem_spec(),
            pl.BlockSpec((cells, LANES), lane),
            pl.BlockSpec((len(OFFSETS), margin, side, LANES), lambda c: (0, 0, 0, c)),
            pl.BlockSpec((taps * taps, LANES), lane),
            pl.BlockSpec((1, LANES), lane),
        ],
        out_specs=[pl.BlockSpec((cells, LANES), lane), pl.BlockSpec((spread, LANES), lane)],
        out_shape=[
            jax.ShapeDtypeStruct((cells, width), F32),
            jax.ShapeDtypeStruct((spread, width), F32),
        ],
        compiler_params=local_params(),
        name="forward_conv",
    )(have, tile, recv, kern, bias)


def backward_kernel(
    side, taps, have_ref, grad_ref, recv_ref, kern_ref, cot_ref, state_ref, out_ref, gkern_ref, padded
):
    margin = taps // 2
    pitch = stride_of(side)

    def center(row):
        return grad_ref[pl.ds(row * side, side), :].astype(BF16).astype(F32)

    place(padded, side, margin, center, have_ref, recv_ref)

    def emit(row, value):
        at = pl.ds(pl.multiple_of(row * side, side), side)
        out_ref[at, :] = (cot_ref[at, :].astype(F32) + value).astype(BF16)

    convolve(padded, kern_ref, side, taps, True, emit)

    group = 4
    for col in range(taps):

        def step(index, sums):
            sums = list(sums)
            base = index * group
            grads = [
                grad_ref[pl.ds(pl.multiple_of((base + out) * side, side), side), :]
                for out in range(group)
            ]
            for row in range(group + taps - 1):
                line = state_ref[pl.ds((base + row) * pitch + (LEAD - margin + col), side), :]
                for out in range(group):
                    up = row - out
                    if 0 <= up < taps:
                        product = line * grads[out]
                        for part in range(side // 8):
                            sums[up] = sums[up] + product[part * 8 : part * 8 + 8]
            return tuple(sums)

        zero = jnp.zeros((8, LANES), F32)
        sums = lax.fori_loop(0, side // group, step, (zero,) * taps)
        for up in range(taps):
            gkern_ref[pl.ds(up * taps + col, 1), :] = jnp.sum(sums[up], axis=0, keepdims=True)


def backward_conv(have, grad, recv, kern, cot, padded, side, taps):
    width = grad.shape[1]
    margin = taps // 2
    cells = side * side
    spread = (side + 2 * margin) * stride_of(side)
    lane = lambda c: (0, c)
    return pl.pallas_call(
        functools.partial(backward_kernel, side, taps),
        grid=(width // LANES,),
        in_specs=[
            smem_spec(),
            pl.BlockSpec((cells, LANES), lane),
            pl.BlockSpec((len(OFFSETS), margin, side, LANES), lambda c: (0, 0, 0, c)),
            pl.BlockSpec((taps * taps, LANES), lane),
            pl.BlockSpec((cells, LANES), lane),
            pl.BlockSpec((spread, LANES), lane),
        ],
        out_specs=[
            pl.BlockSpec((cells, LANES), lane),
            pl.BlockSpec((taps * taps, LANES), lane),
        ],
        out_shape=[
            jax.ShapeDtypeStruct((cells, width), BF16),
            jax.ShapeDtypeStruct((taps * taps, width), F32),
        ],
        scratch_shapes=[pltpu.VMEM((spread, LANES), F32)],
        compiler_params=local_params(),
        name="backward_conv",
    )(have, grad, recv, kern, cot, padded)


def contract_rows(left, right):
    return lax.dot_general(left, right, (((0,), (0,)), ((), ())), preferred_element_type=F32)


def contract_cols(left, right):
    return lax.dot_general(left, right, (((1,), (1,)), ((), ())), preferred_element_type=F32)


def mlp_kernel(
    chunk,
    mixed_ref,
    state_ref,
    cot_ref,
    win_ref,
    wout_ref,
    bin_ref,
    rows_ref,
    new_ref,
    gmix_ref,
    gw_ref,
    gbin_ref,
    gch_ref,
    acc_ref,
):
    step = pl.program_id(0)
    last = pl.num_programs(0) - 1
    hidden = win_ref.shape[1]
    gain = rows_ref[0:1, :]
    shift = rows_ref[1:2, :]
    bout = rows_ref[2:3, :]
    scale = rows_ref[3:4, :]

    @pl.when(step == 0)
    def _():
        acc_ref[...] = jnp.zeros_like(acc_ref)
        gbin_ref[...] = jnp.zeros_like(gbin_ref)
        gch_ref[...] = jnp.zeros_like(gch_ref)

    mixed = mixed_ref[...]
    centered = mixed - jnp.mean(mixed, axis=1, keepdims=True)
    variance = jnp.mean(centered * centered, axis=1, keepdims=True)
    inv_std = lax.rsqrt(variance + EPSILON)
    norm_hat = centered * inv_std
    normed = (norm_hat * gain + shift).astype(BF16)
    cot = cot_ref[...].astype(F32)
    grad_branch = scale * cot
    branch_low = grad_branch.astype(BF16)

    branch = jnp.zeros_like(mixed)
    grad_normed = jnp.zeros_like(mixed)
    for at in range(0, hidden, chunk):
        win = win_ref[:, at : at + chunk]
        wout = wout_ref[at : at + chunk, :]
        pre = jnp.dot(normed, win, preferred_element_type=F32) + bin_ref[:, at : at + chunk]
        square = pre * pre
        tanh_value = jnp.tanh(GELU_SCALE * pre * (1.0 + GELU_CUBIC * square))
        half = 0.5 * (1.0 + tanh_value)
        activation = (pre * half).astype(BF16)
        slope = half + (0.5 * GELU_SCALE) * pre * (1.0 - tanh_value * tanh_value) * (
            1.0 + 3.0 * GELU_CUBIC * square
        )
        grad_pre = contract_cols(branch_low, wout) * slope
        grad_low = grad_pre.astype(BF16)
        branch = branch + jnp.dot(activation, wout, preferred_element_type=F32)
        grad_normed = grad_normed + contract_cols(grad_low, win)
        acc_ref[0, at : at + chunk, :] += contract_rows(grad_low, normed)
        acc_ref[1, at : at + chunk, :] += contract_rows(activation, branch_low)
        gbin_ref[:, at : at + chunk] += jnp.sum(grad_pre, axis=0, keepdims=True)

    branch = branch + bout
    new_ref[...] = (state_ref[...].astype(F32) + scale * branch).astype(BF16)
    scaled = grad_normed * gain
    grad_mixed = inv_std * (
        scaled
        - jnp.mean(scaled, axis=1, keepdims=True)
        - norm_hat * jnp.mean(scaled * norm_hat, axis=1, keepdims=True)
    )
    gmix_ref[...] = grad_mixed
    gch_ref[0:1, :] += jnp.sum(grad_mixed, axis=0, keepdims=True)
    gch_ref[1:2, :] += jnp.sum(grad_normed * norm_hat, axis=0, keepdims=True)
    gch_ref[2:3, :] += jnp.sum(grad_normed, axis=0, keepdims=True)
    gch_ref[3:4, :] += jnp.sum(grad_branch, axis=0, keepdims=True)
    gch_ref[4:5, :] += jnp.sum(cot * branch, axis=0, keepdims=True)

    @pl.when(step == last)
    def _():
        gw_ref[...] = acc_ref[...].astype(BF16)


def pointwise(mixed, state, cot, w_in, w_out, bias_in, rows, block=256, chunk=512):
    cells, width = mixed.shape
    hidden = w_in.shape[1]
    cell = lambda r: (r, 0)
    whole = lambda r: (0, 0)
    return pl.pallas_call(
        functools.partial(mlp_kernel, chunk),
        grid=(cells // block,),
        in_specs=[
            pl.BlockSpec((block, width), cell),
            pl.BlockSpec((block, width), cell),
            pl.BlockSpec((block, width), cell),
            pl.BlockSpec((width, hidden), whole),
            pl.BlockSpec((hidden, width), whole),
            pl.BlockSpec((1, hidden), whole),
            pl.BlockSpec(rows.shape, whole),
        ],
        out_specs=[
            pl.BlockSpec((block, width), cell),
            pl.BlockSpec((block, width), cell),
            pl.BlockSpec((2, hidden, width), lambda r: (0, 0, 0)),
            pl.BlockSpec((1, hidden), whole),
            pl.BlockSpec((8, width), whole),
        ],
        out_shape=[
            jax.ShapeDtypeStruct((cells, width), BF16),
            jax.ShapeDtypeStruct((cells, width), F32),
            jax.ShapeDtypeStruct((2, hidden, width), BF16),
            jax.ShapeDtypeStruct((1, hidden), F32),
            jax.ShapeDtypeStruct((8, width), F32),
        ],
        scratch_shapes=[pltpu.VMEM((2, hidden, width), F32)],
        compiler_params=local_params(),
        name="pointwise",
    )(mixed, state, cot, w_in, w_out, bias_in, rows)


def reduce_kernel(
    members,
    tiles,
    big_ref,
    small_ref,
    out_ref,
    sout_ref,
    core_in,
    x_out,
    x_in,
    t_out,
    t_in,
    own,
    sm_in,
    st_out,
    st_in,
    s_own,
    core_sem,
    x_sem,
    t_sem,
    g_sem,
    sm_sem,
    st_sem,
    sg_sem,
):
    member = lax.axis_index("member")
    tile = lax.axis_index("tile")
    core = lax.rem(member, 2)
    cross = member // 2
    spots = members // 2
    mates = [lax.rem(member + k, members) for k in range(1, members)]
    peers = [lax.rem(tile + k, tiles) for k in range(1, tiles)]
    barrier = pltpu.get_barrier_semaphore()
    for mate in mates:
        pl.semaphore_signal(barrier, inc=1, device_id={"member": mate}, device_id_type=MESH)
    for peer in peers:
        pl.semaphore_signal(barrier, inc=1, device_id={"tile": peer}, device_id_type=MESH)
    pl.semaphore_wait(barrier, members + tiles - 2)

    def remote(source, target, sems, slot, **device):
        copy = pltpu.make_async_remote_copy(
            src_ref=source,
            dst_ref=target,
            send_sem=sems.at[0, slot],
            recv_sem=sems.at[1, slot],
            device_id=device,
            device_id_type=MESH,
        )
        copy.start()
        return copy

    pair = [
        remote(big_ref.at[:, :, :, 1 - core], core_in, core_sem, 0, member=cross * 2 + 1 - core)
    ]
    small = [
        remote(small_ref, sm_in.at[k], sm_sem, k, member=mate) for k, mate in enumerate(mates)
    ]
    pair[0].wait()

    def add_pair(t, carry):
        for x in range(spots):
            x_out[x, :, t] = (
                big_ref[:, t, x, core].astype(F32) + core_in[:, t, x].astype(F32)
            ).astype(BF16)
        return carry

    lax.fori_loop(0, tiles, add_pair, 0)
    over = []
    for k in range(1, spots):
        spot = lax.rem(cross + k, spots)
        over.append(remote(x_out.at[spot], x_in.at[k - 1], x_sem, k - 1, member=spot * 2 + core))
    for copy in small:
        copy.wait()
    total = small_ref[...]
    for k in range(members - 1):
        total = total + sm_in[k]
    st_out[...] = total
    small = [
        remote(st_out.at[peer], st_in.at[k], st_sem, k, tile=peer) for k, peer in enumerate(peers)
    ]
    for copy in over:
        copy.wait()

    def add_cross(t, carry):
        value = x_out[cross, :, t].astype(F32)
        for k in range(spots - 1):
            value = value + x_in[k, :, t].astype(F32)
        t_out[t] = value.astype(BF16)
        return carry

    lax.fori_loop(0, tiles, add_cross, 0)
    along = [
        remote(t_out.at[peer], t_in.at[k], t_sem, k, tile=peer) for k, peer in enumerate(peers)
    ]
    for copy in small:
        copy.wait()
    total = st_out[tile]
    for k in range(tiles - 1):
        total = total + st_in[k]
    s_own[...] = total
    small = [
        remote(s_own, sout_ref.at[tile], sg_sem, k, tile=peer) for k, peer in enumerate(peers)
    ]
    sout_ref[tile] = total
    for copy in along:
        copy.wait()
    value = t_out[tile].astype(F32)
    for k in range(tiles - 1):
        value = value + t_in[k].astype(F32)
    own[...] = value.astype(BF16)
    back = [
        remote(own, out_ref.at[member], g_sem, k, member=mate) for k, mate in enumerate(mates)
    ]
    out_ref[member] = own[...]
    for copy in small + back:
        copy.wait()


def reduce_all(big, small, members, tiles):
    _, _, spots, _, rows, width = big.shape
    lines = small.shape[1]
    dma = lambda n: pltpu.SemaphoreType.DMA((2, max(n, 1)))
    return pl.pallas_call(
        functools.partial(reduce_kernel, members, tiles),
        in_specs=[vmem_spec(), vmem_spec()],
        out_specs=[vmem_spec(), vmem_spec()],
        out_shape=[
            jax.ShapeDtypeStruct((members, 2, rows, width), BF16),
            jax.ShapeDtypeStruct((tiles, lines, width), F32),
        ],
        scratch_shapes=[
            pltpu.VMEM((2, tiles, spots, rows, width), BF16),
            pltpu.VMEM((spots, 2, tiles, rows, width), BF16),
            pltpu.VMEM((max(spots - 1, 1), 2, tiles, rows, width), BF16),
            pltpu.VMEM((tiles, 2, rows, width), BF16),
            pltpu.VMEM((tiles - 1, 2, rows, width), BF16),
            pltpu.VMEM((2, rows, width), BF16),
            pltpu.VMEM((members - 1, tiles, lines, width), F32),
            pltpu.VMEM((tiles, lines, width), F32),
            pltpu.VMEM((tiles - 1, lines, width), F32),
            pltpu.VMEM((lines, width), F32),
            dma(1),
            dma(spots - 1),
            dma(tiles - 1),
            dma(members - 1),
            dma(members - 1),
            dma(tiles - 1),
            dma(tiles - 1),
        ],
        compiler_params=pltpu.CompilerParams(
            collective_id=2, has_side_effects=True, vmem_limit_bytes=VMEM_LIMIT
        ),
        name="reduce_all",
    )(big, small)


def body(
    state,
    cotangent,
    neighbors,
    kernel,
    conv_bias,
    norm_gain,
    norm_shift,
    w_in,
    bias_in,
    w_out,
    bias_out,
    layer_scale,
):
    side, width = state.shape[2], state.shape[4]
    cells = side * side
    center = state.reshape(cells, width)
    cot = cotangent.reshape(cells, width)
    hidden = w_in.shape[1]
    taps = kernel.shape[0]
    margin = taps // 2
    count = lax.axis_size("tile")
    members = lax.axis_size("member")
    myself = lax.axis_index("tile")
    steps = jnp.array(OFFSETS, jnp.int32)
    takers = (myself + steps + count) % count
    givers = (myself - steps + count) % count
    want = (neighbors[takers] == myself).astype(jnp.int32)
    have = (neighbors[myself][None, :] == givers[:, None]).astype(jnp.int32)
    flat_kernel = kernel.reshape(taps * taps, width)

    got = exchange(payload(want, center, side, margin), count, 0)
    mixed, padded = forward_conv(have, center, got, flat_kernel, conv_bias[None], side, taps)
    vectors = jnp.stack([norm_gain, norm_shift, bias_out, layer_scale] * 2)
    new_tile, grad_mixed, grad_w, grad_bin, grad_ch = pointwise(
        mixed, center, cot, w_in, w_out, bias_in[None], vectors
    )
    got_grad = exchange(payload(want, grad_mixed, side, margin), count, 1)
    state_grad, grad_kern = backward_conv(
        have, grad_mixed, got_grad, flat_kernel, cot, padded, side, taps
    )

    share = hidden // count
    rows = share // members
    big = grad_w.reshape(2, count, members // 2, 2, rows, width)
    parts = [grad_kern, grad_bin.reshape(hidden // width, width), grad_ch]
    packed = jnp.concatenate(parts, axis=0)
    lines = 8 * (-(-packed.shape[0] // (8 * count)))
    packed = jnp.pad(packed, ((0, lines * count - packed.shape[0]), (0, 0)))
    big, small = reduce_all(big, packed.reshape(count, lines, width), members, count)
    factor = 1.0 / math.sqrt(members * count * cells)
    big = big.astype(F32) * factor
    win_share = big[:, 0].reshape(share, width).T
    wout_share = big[:, 1].reshape(share, width)
    small = small.reshape(count * lines, width) * factor
    first = taps * taps
    second = first + hidden // width
    return (
        new_tile.reshape(state.shape),
        state_grad.reshape(state.shape),
        win_share,
        wout_share,
        small[:first].reshape(taps, taps, width),
        small[first:second].reshape(hidden),
        small[second : second + 5],
    )


def solution(mesh):
    tiled = P("member", "tile", None, None, None)
    in_specs = (tiled, tiled) + (P(),) * 10
    out_specs = (tiled, tiled, P(None, "tile"), P("tile", None), P(), P(), P())
    return jax.shard_map(body, mesh=mesh, in_specs=in_specs, out_specs=out_specs, check_vma=False)
```

time: 405 us -> 149 us (0.37)
  Pallas kernels: 0 us -> 129 us
  other arithmetic: 125 us -> 6.12 us
  waiting for transfers between devices: 113 us -> 0 us
  local copies, waits for them, and re-layouts: 58.3 us -> 11.4 us
  blocking collectives: 39.4 us -> 0 us
  starting transfers between devices: 28.4 us -> 0 us
  matrix products: 21.8 us -> 0 us
  between operations: 15.9 us -> 0.72 us
    pallas_call x0 -> x8, Pallas kernels: none -> 129 us  [the longest x1 42.8 us: reduce_all(): pl.pallas_call(functools.partial(reduce_kernel, members, tiles), in_specs...]
    psum x1 -> x0, waiting for transfers between devices: 80.3 us -> none  [body(): lax.psum((grad_win, grad_bin, grad_kern, grad_conv, grad_gain, grad_shift...]
    select_n x13 -> x1, other arithmetic: 50 us -> 0.68 us  [body(): want = (neighbors[takers] == myself).astype(jnp.int32)]
    another operation x63 -> x5, local copies, waits for them, and re-layouts: 46.1 us -> 3.35 us  [body(): vectors = jnp.stack([norm_gain, norm_shift, bias_out, layer_scale] * 2)]
    psum x1 -> x0, blocking collectives: 39.4 us -> none  [body(): lax.psum((grad_win, grad_bin, grad_kern, grad_conv, grad_gain, grad_shift...]
    ppermute x12 -> x0, waiting for transfers between devices: 33.2 us -> none  [shifted(): return lax.ppermute(value, axis, pairs)]
    reduce_sum x7 -> x0, other arithmetic: 30.2 us -> none  [the longest x3 13.9 us: kernel_grad(): line.append(jnp.sum(window * grad_mixed, axis=(0, 1)))]
    ppermute x12 -> x0, starting transfers between devices: 28.3 us -> none  [shifted(): return lax.ppermute(value, axis, pairs)]
  transfers between devices with their start and end apart: 13 -> 0, of which waited for: 3 -> 0; matrix products, arithmetic and copies ran while one was open for 26% -> 0% of each run, Pallas kernels for 0% -> 0%
where the time goes in v1:
time: 149 us; the launch traced here: 147 us
  Pallas kernels  129 us (87%)
  local copies, waits for them, and re-layouts  11.4 us (8%)
  other arithmetic  6.12 us (4%)
    pallas_call x1, Pallas kernels, reduce_all(): pl.pallas_call(functools.partial(reduce_kernel, members, tiles), in_specs...  42.8 us
    pallas_call x2, Pallas kernels, exchange(): pl.pallas_call(functools.partial(exchange_kernel, count), in_specs=[vmem_...  31.5 us
    pallas_call x1, Pallas kernels, pointwise(): pl.pallas_call(functools.partial(mlp_kernel, chunk), grid=(cells // block...  18.8 us
    pallas_call x1, Pallas kernels, backward_conv(): pl.pallas_call(functools.partial(backward_kernel, side, taps), grid=(widt...  15.7 us
    pallas_call x1, Pallas kernels, forward_conv(): pl.pallas_call(functools.partial(forward_kernel, side, taps), grid=(width...  12.6 us
    pallas_call x2, Pallas kernels, payload(): pl.pallas_call(functools.partial(payload_kernel, side, margin), grid=(wid...  7.31 us
    another operation x5, local copies, waits for them, and re-layouts, body(): vectors = jnp.stack([norm_gain, norm_shift, bias_out, layer_scale] * 2)  3.35 us

profile of v1, /device:TPU:0, one launch (start us, length us, event | category | flops | bytes accessed | tf_op | source)
XLA Modules:
  0.0 147.0 jit_solution(621496394830793674)
XLA Ops:
  0.6 0.0 copy-start
  0.7 0.7 copy-done
  1.3 0.7 compare_select_fusion
  2.0 1.2 broadcast_in_dim.11.bias_ref
  3.3 0.7 stack.19
  3.9 0.7 stack.20
  4.6 0.7 stack.21
  5.3 0.7 stack.22
  6.0 0.7 compare_convert_fusion.1.have_ref
  6.7 0.6 gather_fusion
  7.2 0.6 compare_convert_fusion.want_ref
  7.8 0.6 stack.23.rows_ref
  8.4 1.3 broadcast_in_dim.12.bin_ref
  9.7 1.5 %reshape.49.kern_ref = f32[49,384]{1,0:T(8,128)} reshape(f32[7,7,384]{2,1,0:T(8,128)} %param.16) | data formatting | bytes 150528 | tf_op jit(solution)/shard_map/reshape | solution.py:600
  11.3 3.6 %payload.2.send_ref = bf16[6,3,32,384]{3,2,1,0:T(8,128)(2,1)} custom-call(s32[6,8]{1,0:T(8,128)} %compare_convert_fusion.want_ref, bf16[1024,384]{1,0:T(8,128)(2,1)} %bitcast.15), custom_call_target="tpu_custom_call" | custom-call | tf_op jit(solution)/shard_map/payload/pallas_call | solution.py:63
  14.8 16.6 %exchange.2.recv_ref = bf16[6,3,32,384]{3,2,1,0:T(8,128)(2,1)} custom-call(bf16[6,3,32,384]{3,2,1,0:T(8,128)(2,1)} %payload.2.send_ref), custom_call_target="tpu_custom_call" | custom-call | tf_op jit(solution)/shard_map/exchange/pallas_call | solution.py:99
  31.5 12.6 %forward_conv.1 = (f32[1024,384]{1,0:T(8,128)}, f32[1824,384]{1,0:T(8,128)}) custom-call(s32[6,8]{1,0:T(8,128)} %compare_convert_fusion.1.have_ref, bf16[1024,384]{1,0:T(8,128)(2,1)} %bitcast.16, bf16[6,3,32,384]{3,2,1,0:T(8,128)(2,1)} %exchange.2.recv_ref, f32[49,384]{1,0:T(8,128)} %reshape.49.kern_ref, f32[1,384]{1,0:T(1,128)} %broadcast_in_dim.11.bias_ref), custom_call_target="tpu_custom_call" | custom-call | tf_op jit(solution)/shard_map/forward_conv/pallas_call | solution.py:195
  44.1 18.8 %pointwise.1 = (bf16[1024,384]{1,0:T(8,128)(2,1)}, f32[1024,384]{1,0:T(8,128)}, bf16[2,1536,384]{2,1,0:T(8,128)(2,1)}, f32[1,1536]{1,0:T(1,128)}, f32[8,384]{1,0:T(8,128)}) custom-call(f32[1024,384]{1,0:T(8,128)} %get-tuple-element.18.mixed_ref, bf16[1024,384]{1,0:T(8,128)(2,1)} %bitcast.17, bf16[1024,384]{1,0:T(8,128)(2,1)} %bitcast.18, ...), custom_call_target="tpu_custom_call" | custom-call | tf_op jit(solution)/shard_map/pointwise/pallas_call | solution.py:383
  62.9 0.7 reduce
  63.6 3.8 %payload.3.send_ref = bf16[6,3,32,384]{3,2,1,0:T(8,128)(2,1)} custom-call(s32[6,8]{1,0:T(8,128)} %compare_convert_fusion.want_ref, f32[1024,384]{1,0:T(8,128)} %get-tuple-element.20.tile_ref.grad_ref), custom_call_target="tpu_custom_call" | custom-call | tf_op jit(solution)/shard_map/payload/pallas_call | solution.py:63
  67.4 14.9 %exchange.3.recv_ref = bf16[6,3,32,384]{3,2,1,0:T(8,128)(2,1)} custom-call(bf16[6,3,32,384]{3,2,1,0:T(8,128)(2,1)} %payload.3.send_ref), custom_call_target="tpu_custom_call" | custom-call | tf_op jit(solution)/shard_map/exchange/pallas_call | solution.py:99
  82.2 0.0 copy-start.1
  82.2 15.7 %backward_conv.1 = (bf16[1024,384]{1,0:T(8,128)(2,1)}, f32[49,384]{1,0:T(8,128)}) custom-call(s32[6,8]{1,0:T(8,128)} %compare_convert_fusion.1.have_ref, f32[1024,384]{1,0:T(8,128)} %get-tuple-element.20.tile_ref.grad_ref, bf16[6,3,32,384]{3,2,1,0:T(8,128)(2,1)} %exchange.3.recv_ref, f32[49,384]{1,0:T(8,128)} %reshape.49.kern_ref, ...), custom_call_target="tpu_custom_call" | custom-call | tf_op jit(solution)/shard_map/backward_conv/pallas_call | solution.py:264
  98.0 0.0 copy-done.1
  98.0 1.5 %fusion.small_ref = f32[8,8,384]{2,1,0:T(8,128)} fusion(f32[8,384]{1,0:T(8,128)S(1)} %copy-done.1, f32[4,384]{1,0:T(4,128)S(1)} %reshape.54, f32[49,384]{1,0:T(8,128)} %get-tuple-element.24), kind=kLoop, calls=%fused_computation.3 | loop fusion | flops 147456 | bytes 192000 | tf_op jit(solution)/shard_map/reshape | solution.py:620
  99.5 42.8 %reduce_all.1 = (bf16[4,2,48,384]{3,2,1,0:T(8,128)(2,1)}, f32[8,8,384]{2,1,0:T(8,128)}) custom-call(bf16[2,8,2,2,48,384]{5,4,3,2,1,0:T(8,128)(2,1)} %bitcast.20, f32[8,8,384]{2,1,0:T(8,128)} %fusion.small_ref), custom_call_target="tpu_custom_call" | custom-call | tf_op jit(solution)/shard_map/reduce_all/pallas_call | solution.py:537
  142.3 0.9 multiply_bitcast_fusion
  143.3 0.6 reshape.57
  143.9 0.6 slice.26
  144.5 0.6 reshape.56
  145.1 1.0 convert_multiply_fusion
  146.1 0.9 fusion.3
  (5 shorter events, 0.0 us)
Async XLA Ops:
  0.6 0.7 copy-start
  82.2 15.8 %copy-start.1 = (f32[8,384]{1,0:T(8,128)S(1)}, f32[8,384]{1,0:T(8,128)}, u32[]{:S(2)}) copy-start(f32[8,384]{1,0:T(8,128)} %get-tuple-element.26) | copy-start | bytes 36868

commit v2 on v1

v2 whole, which is shorter than its diff:
```python
import functools
import math

import jax
import jax.numpy as jnp
from jax import lax
from jax.experimental import pallas as pl
from jax.experimental.pallas import tpu as pltpu
from jax.sharding import PartitionSpec as P

OFFSETS = (1, 2, 3, -1, -2, -3)
GELU_SCALE = 0.7978845608028654
GELU_CUBIC = 0.044715
EPSILON = 1e-06
LANES = 128
LEAD = 8
MESH = pl.DeviceIdType.MESH
F32 = jnp.float32
BF16 = jnp.bfloat16
VMEM_LIMIT = 56 << 20


def vmem_spec():
    return pl.BlockSpec(memory_space=pltpu.VMEM)


def smem_spec():
    return pl.BlockSpec(memory_space=pltpu.SMEM)


def local_params():
    return pltpu.CompilerParams(vmem_limit_bytes=VMEM_LIMIT)


def remote_params(ident):
    return pltpu.CompilerParams(
        collective_id=ident, has_side_effects=True, vmem_limit_bytes=VMEM_LIMIT
    )


def pitch_of(side):
    return side + 2 * LEAD


def spread_of(side, margin):
    return (side + 2 * margin) * pitch_of(side)


def place(padded, side, margin, center):
    pitch = pitch_of(side)
    for part in range(padded.shape[0]):

        def clear(row, carry):
            at = pl.ds(pl.multiple_of(row * pitch, 8), pitch)
            padded[part, at, :] = jnp.zeros((pitch, LANES), F32)
            return carry

        lax.fori_loop(0, side + 2 * margin, clear, 0)

        def put(row, carry):
            at = pl.ds(pl.multiple_of((margin + row) * pitch + LEAD, 8), side)
            padded[part, at, :] = center(part, row)
            return carry

        lax.fori_loop(0, side, put, 0)


def around(tile, count):
    takers = [lax.rem(tile + offset + count, count) for offset in OFFSETS]
    givers = [lax.rem(tile - offset + count, count) for offset in OFFSETS]
    return takers, givers


def pack(padded, side, margin, want, send_ref):
    pitch = pitch_of(side)
    edge = side - margin
    for part in range(padded.shape[0]):
        lanes = pl.ds(part * LANES, LANES)
        for k in range(margin):
            low = (margin + k) * pitch + LEAD
            high = (margin + edge + k) * pitch + LEAD
            first = margin * pitch + LEAD
            lines = [
                padded[part, pl.ds(low, side), :],
                padded[part, pl.ds(high, side), :],
                padded[part, pl.ds(first + k, side, stride=pitch), :],
                padded[part, pl.ds(first + edge + k, side, stride=pitch), :],
            ]
            lines = lines + [
                jnp.concatenate([lines[0][:8]] * (side // 8), axis=0),
                jnp.concatenate([lines[0][side - 8 :]] * (side // 8), axis=0),
                jnp.concatenate([lines[1][:8]] * (side // 8), axis=0),
                jnp.concatenate([lines[1][side - 8 :]] * (side // 8), axis=0),
            ]
            for slot in range(len(OFFSETS)):
                line = lines[7]
                for way in range(7):
                    line = jnp.where(want[slot][way], lines[way], line)
                send_ref[slot, k, :, lanes] = line.astype(BF16)


def unpack(padded, side, margin, have, recv_ref):
    pitch = pitch_of(side)
    for part in range(padded.shape[0]):
        lanes = pl.ds(part * LANES, LANES)
        for k in range(margin):
            lines = [recv_ref[slot, k, :, lanes].astype(F32) for slot in range(len(OFFSETS))]
            for way in range(8):
                size = side if way < 4 else 8
                line = jnp.zeros((size, LANES), F32)
                for slot in range(len(OFFSETS)):
                    line = jnp.where(have[slot][way], lines[slot][:size], line)
                if way == 0:
                    at = pl.ds((margin + side + k) * pitch + LEAD, side)
                elif way == 1:
                    at = pl.ds(k * pitch + LEAD, side)
                elif way == 2:
                    at = pl.ds(margin * pitch + LEAD + side + k, side, stride=pitch)
                elif way == 3:
                    at = pl.ds(margin * pitch + LEAD - margin + k, side, stride=pitch)
                else:
                    row = margin + side + k if way in (4, 5) else k
                    at = pl.ds(row * pitch + (LEAD + side if way in (4, 6) else LEAD - 8), 8)
                padded[part, at, :] = line


def convolve(padded, part, kern_ref, side, taps, flipped, emit, group=4):
    pitch = pitch_of(side)
    margin = taps // 2
    lanes = pl.ds(part * LANES, LANES)

    def step(index, carry):
        base = index * group
        total = [jnp.zeros((side, LANES), F32) for _ in range(group)]
        for col in range(taps):
            for row in range(group + taps - 1):
                start = (base + row) * pitch
                line = padded[part, pl.ds(start + (LEAD - margin + col), side), :]
                for out in range(group):
                    up = row - out
                    if 0 <= up < taps:
                        a, b = (taps - 1 - up, taps - 1 - col) if flipped else (up, col)
                        total[out] = total[out] + kern_ref[a, pl.ds(b, 1), lanes] * line
        for out in range(group):
            emit(pl.multiple_of((base + out) * side, side), total[out])
        return carry

    lax.fori_loop(0, side // group, step, 0)


def kernel_grad(padded, part, grad_ref, side, taps, emit, group=4):
    pitch = pitch_of(side)
    margin = taps // 2
    for col in range(taps):

        def step(index, sums):
            sums = list(sums)
            base = index * group
            grads = [
                grad_ref[part, pl.ds(pl.multiple_of((base + out) * side, side), side), :]
                for out in range(group)
            ]
            for row in range(group + taps - 1):
                start = (base + row) * pitch
                line = padded[part, pl.ds(start + (LEAD - margin + col), side), :]
                for out in range(group):
                    up = row - out
                    if 0 <= up < taps:
                        product = line * grads[out]
                        for piece in range(side // 8):
                            sums[up] = sums[up] + product[piece * 8 : piece * 8 + 8]
            return tuple(sums)

        zero = jnp.zeros((8, LANES), F32)
        sums = lax.fori_loop(0, side // group, step, (zero,) * taps)
        for up in range(taps):
            emit(up, col, jnp.sum(sums[up], axis=0, keepdims=True))


def remote(source, target, sems, slot, **device):
    copy = pltpu.make_async_remote_copy(
        src_ref=source,
        dst_ref=target,
        send_sem=sems.at[0, slot],
        recv_sem=sems.at[1, slot],
        device_id=device,
        device_id_type=MESH,
    )
    copy.start()
    return copy


def swap_halo(padded, side, margin, links_ref, send_ref, recv_ref, sems, count, ready):
    tile = lax.axis_index("tile")
    takers, _ = around(tile, count)
    want = [[links_ref[taker, way] == tile for way in range(8)] for taker in takers]
    pack(padded, side, margin, want, send_ref)
    ready()
    return [
        remote(send_ref.at[slot], recv_ref.at[slot], sems, slot, tile=taker)
        for slot, taker in enumerate(takers)
    ]


def take_halo(padded, side, margin, links_ref, recv_ref, count):
    tile = lax.axis_index("tile")
    _, givers = around(tile, count)
    have = [[links_ref[tile, way] == giver for way in range(8)] for giver in givers]
    unpack(padded, side, margin, have, recv_ref)


def forward_kernel(
    side, taps, count, links_ref, tile_ref, kern_ref, bias_ref, mixed_ref, padded, send, recv, sems
):
    margin = taps // 2
    barrier = pltpu.get_barrier_semaphore()
    takers, _ = around(lax.axis_index("tile"), count)
    for taker in takers:
        pl.semaphore_signal(barrier, inc=1, device_id={"tile": taker}, device_id_type=MESH)

    def center(part, row):
        at = pl.ds(pl.multiple_of(row * side, side), side)
        return tile_ref[at, pl.ds(part * LANES, LANES)].astype(F32)

    place(padded, side, margin, center)
    copies = swap_halo(
        padded, side, margin, links_ref, send, recv, sems, count,
        lambda: pl.semaphore_wait(barrier, len(OFFSETS)),
    )
    for copy in copies:
        copy.wait()
    take_halo(padded, side, margin, links_ref, recv, count)
    for part in range(padded.shape[0]):
        lanes = pl.ds(part * LANES, LANES)
        bias = bias_ref[lanes].reshape(1, LANES)

        def emit(start, value):
            mixed_ref[pl.ds(start, side), lanes] = value + bias

        convolve(padded, part, kern_ref, side, taps, False, emit)


def halo_scratch(side, margin, width):
    pieces = (len(OFFSETS), margin, side, width)
    return [
        pltpu.VMEM(pieces, BF16),
        pltpu.VMEM(pieces, BF16),
        pltpu.SemaphoreType.DMA((2, len(OFFSETS))),
    ]


def forward_conv(links, tile, kern, bias, side, taps, count):
    cells, width = tile.shape
    margin = taps // 2
    return pl.pallas_call(
        functools.partial(forward_kernel, side, taps, count),
        in_specs=[smem_spec()] + [vmem_spec()] * 3,
        out_specs=[vmem_spec()] * 2,
        out_shape=[
            jax.ShapeDtypeStruct((cells, width), F32),
            jax.ShapeDtypeStruct((width // LANES, spread_of(side, margin), LANES), F32),
        ],
        scratch_shapes=halo_scratch(side, margin, width),
        compiler_params=remote_params(0),
        name="forward_conv",
    )(links, tile, kern, bias)


def contract_rows(left, right):
    return lax.dot_general(left, right, (((0,), (0,)), ((), ())), preferred_element_type=F32)


def contract_cols(left, right):
    return lax.dot_general(left, right, (((1,), (1,)), ((), ())), preferred_element_type=F32)


def mlp_kernel(
    chunk,
    mixed_ref,
    state_ref,
    cot_ref,
    win_ref,
    wout_ref,
    bin_ref,
    gain_ref,
    shift_ref,
    bout_ref,
    scale_ref,
    new_ref,
    gmix_ref,
    gw_ref,
    gbin_ref,
    gch_ref,
    acc_ref,
):
    step = pl.program_id(0)
    last = pl.num_programs(0) - 1
    hidden = win_ref.shape[1]
    gain, shift, bout, scale = (
        ref[...].reshape(1, -1) for ref in (gain_ref, shift_ref, bout_ref, scale_ref)
    )

    @pl.when(step == 0)
    def _():
        acc_ref[...] = jnp.zeros_like(acc_ref)
        gbin_ref[...] = jnp.zeros_like(gbin_ref)
        gch_ref[...] = jnp.zeros_like(gch_ref)

    mixed = mixed_ref[...]
    centered = mixed - jnp.mean(mixed, axis=1, keepdims=True)
    variance = jnp.mean(centered * centered, axis=1, keepdims=True)
    inv_std = lax.rsqrt(variance + EPSILON)
    norm_hat = centered * inv_std
    normed = (norm_hat * gain + shift).astype(BF16)
    cot = cot_ref[...].astype(F32)
    grad_branch = scale * cot
    branch_low = grad_branch.astype(BF16)

    branch = jnp.zeros_like(mixed)
    grad_normed = jnp.zeros_like(mixed)
    for at in range(0, hidden, chunk):
        win = win_ref[:, at : at + chunk]
        wout = wout_ref[at : at + chunk, :]
        pre = jnp.dot(normed, win, preferred_element_type=F32) + bin_ref[pl.ds(at, chunk)].reshape(1, chunk)
        square = pre * pre
        tanh_value = jnp.tanh(GELU_SCALE * pre * (1.0 + GELU_CUBIC * square))
        half = 0.5 * (1.0 + tanh_value)
        activation = (pre * half).astype(BF16)
        slope = half + (0.5 * GELU_SCALE) * pre * (1.0 - tanh_value * tanh_value) * (
            1.0 + 3.0 * GELU_CUBIC * square
        )
        grad_pre = contract_cols(branch_low, wout) * slope
        grad_low = grad_pre.astype(BF16)
        branch = branch + jnp.dot(activation, wout, preferred_element_type=F32)
        grad_normed = grad_normed + contract_cols(grad_low, win)
        acc_ref[0, at : at + chunk, :] += contract_rows(grad_low, normed)
        acc_ref[1, at : at + chunk, :] += contract_rows(activation, branch_low)
        gbin_ref[:, at : at + chunk] += jnp.sum(grad_pre, axis=0, keepdims=True)

    branch = branch + bout
    new_ref[...] = (state_ref[...].astype(F32) + scale * branch).astype(BF16)
    scaled = grad_normed * gain
    grad_mixed = inv_std * (
        scaled
        - jnp.mean(scaled, axis=1, keepdims=True)
        - norm_hat * jnp.mean(scaled * norm_hat, axis=1, keepdims=True)
    )
    for part in range(gmix_ref.shape[0]):
        gmix_ref[part] = grad_mixed[:, part * LANES : (part + 1) * LANES]
    gch_ref[0:1, :] += jnp.sum(grad_mixed, axis=0, keepdims=True)
    gch_ref[1:2, :] += jnp.sum(grad_normed * norm_hat, axis=0, keepdims=True)
    gch_ref[2:3, :] += jnp.sum(grad_normed, axis=0, keepdims=True)
    gch_ref[3:4, :] += jnp.sum(grad_branch, axis=0, keepdims=True)
    gch_ref[4:5, :] += jnp.sum(cot * branch, axis=0, keepdims=True)

    @pl.when(step == last)
    def _():
        gw_ref[...] = acc_ref[...].astype(BF16)


def pointwise(mixed, state, cot, w_in, w_out, bias_in, vectors, block=256, chunk=512):
    cells, width = mixed.shape
    hidden = w_in.shape[1]
    cell = lambda r: (r, 0)
    whole = lambda r: (0, 0)
    return pl.pallas_call(
        functools.partial(mlp_kernel, chunk),
        grid=(cells // block,),
        in_specs=[
            pl.BlockSpec((block, width), cell),
            pl.BlockSpec((block, width), cell),
            pl.BlockSpec((block, width), cell),
            pl.BlockSpec((width, hidden), whole),
            pl.BlockSpec((hidden, width), whole),
            pl.BlockSpec((hidden,), lambda r: (0,)),
        ]
        + [pl.BlockSpec((width,), lambda r: (0,))] * 4,
        out_specs=[
            pl.BlockSpec((block, width), cell),
            pl.BlockSpec((width // LANES, block, LANES), lambda r: (0, r, 0)),
            pl.BlockSpec((2, hidden, width), lambda r: (0, 0, 0)),
            pl.BlockSpec((1, hidden), whole),
            pl.BlockSpec((8, width), whole),
        ],
        out_shape=[
            jax.ShapeDtypeStruct((cells, width), BF16),
            jax.ShapeDtypeStruct((width // LANES, cells, LANES), F32),
            jax.ShapeDtypeStruct((2, hidden, width), BF16),
            jax.ShapeDtypeStruct((1, hidden), F32),
            jax.ShapeDtypeStruct((8, width), F32),
        ],
        scratch_shapes=[pltpu.VMEM((2, hidden, width), F32)],
        compiler_params=local_params(),
        name="pointwise",
    )(mixed, state, cot, w_in, w_out, bias_in, *vectors)


def backward_kernel(
    side,
    taps,
    members,
    tiles,
    links_ref,
    grad_ref,
    kern_ref,
    cot_ref,
    state_ref,
    gbin_ref,
    gch_ref,
    big_ref,
    sgrad_ref,
    out_ref,
    sout_ref,
    padded,
    send,
    recv,
    sems,
    core_in,
    x_out,
    x_in,
    t_out,
    t_in,
    own,
    s_pack,
    sm_in,
    st_out,
    st_in,
    s_own,
    core_sem,
    x_sem,
    t_sem,
    g_sem,
    sm_sem,
    st_sem,
    sg_sem,
):
    margin = taps // 2
    parts = padded.shape[0]
    member = lax.axis_index("member")
    tile = lax.axis_index("tile")
    core = lax.rem(member, 2)
    cross = member // 2
    spots = members // 2
    mates = [lax.rem(member + k, members) for k in range(1, members)]
    peers = [lax.rem(tile + k, tiles) for k in range(1, tiles)]
    barrier = pltpu.get_barrier_semaphore()
    for mate in mates:
        pl.semaphore_signal(barrier, inc=1, device_id={"member": mate}, device_id_type=MESH)
    for peer in peers:
        pl.semaphore_signal(barrier, inc=1, device_id={"tile": peer}, device_id_type=MESH)

    def center(part, row):
        at = pl.ds(pl.multiple_of(row * side, side), side)
        return grad_ref[part, at, :].astype(BF16).astype(F32)

    place(padded, side, margin, center)
    halo = swap_halo(
        padded, side, margin, links_ref, send, recv, sems, tiles,
        lambda: pl.semaphore_wait(barrier, members + tiles - 2),
    )
    pair = [
        remote(
            big_ref.at[kind, :, :, 1 - core], core_in.at[kind], core_sem, kind,
            member=cross * 2 + 1 - core,
        )
        for kind in range(2)
    ]

    lines = s_pack.shape[1]
    s_pack[...] = jnp.zeros_like(s_pack)
    width = s_pack.shape[2]
    first = taps * taps
    extra = gbin_ref.shape[1] // width
    for row in range(extra):
        at = first + row
        s_pack[at // lines, pl.ds(at % lines, 1), :] = gbin_ref[:, pl.ds(row * width, width)]
    for row in range(5):
        at = first + extra + row
        s_pack[at // lines, pl.ds(at % lines, 1), :] = gch_ref[pl.ds(row, 1), :]

    def own_kernel(part):
        def emit(up, col, value):
            at = up * taps + col
            s_pack[at // lines, pl.ds(at % lines, 1), pl.ds(part * LANES, LANES)] = value

        kernel_grad(state_ref, part, grad_ref, side, taps, emit)

    def conv(part):
        lanes = pl.ds(part * LANES, LANES)

        def emit(start, value):
            at = pl.ds(start, side)
            sgrad_ref[at, lanes] = (cot_ref[at, lanes].astype(F32) + value).astype(BF16)

        convolve(padded, part, kern_ref, side, taps, True, emit)

    def cross_over(kind):
        pair[kind].wait()

        def add(t, carry):
            for x in range(spots):
                mine = big_ref[kind, t, x, core].astype(F32)
                x_out[kind, x, t] = (mine + core_in[kind, t, x].astype(F32)).astype(BF16)
            return carry

        lax.fori_loop(0, tiles, add, 0)
        copies = []
        for k in range(1, spots):
            spot = lax.rem(cross + k, spots)
            copies.append(
                remote(
                    x_out.at[kind, spot], x_in.at[kind, k - 1], x_sem, kind * (spots - 1) + k - 1,
                    member=spot * 2 + core,
                )
            )
        return copies

    def go_along(kind, copies):
        for copy in copies:
            copy.wait()

        def add(t, carry):
            value = x_out[kind, cross, t].astype(F32)
            for k in range(spots - 1):
                value = value + x_in[kind, k, t].astype(F32)
            t_out[kind, t] = value.astype(BF16)
            return carry

        lax.fori_loop(0, tiles, add, 0)
        return [
            remote(
                t_out.at[kind, peer], t_in.at[kind, k], t_sem, kind * (tiles - 1) + k, tile=peer
            )
            for k, peer in enumerate(peers)
        ]

    def send_back(kind, copies):
        for copy in copies:
            copy.wait()
        value = t_out[kind, tile].astype(F32)
        for k in range(tiles - 1):
            value = value + t_in[kind, k].astype(F32)
        own[kind] = value.astype(BF16)
        out_ref[kind, member] = value.astype(BF16)
        return [
            remote(
                own.at[kind], out_ref.at[kind, member], g_sem, kind * (members - 1) + k, member=mate
            )
            for k, mate in enumerate(mates)
        ]

    own_kernel(0)
    over = [cross_over(0)]
    own_kernel(1)
    over.append(cross_over(1))
    for part in range(2, parts):
        own_kernel(part)
    small = [remote(s_pack, sm_in.at[k], sm_sem, k, member=mate) for k, mate in enumerate(mates)]
    for copy in halo:
        copy.wait()
    take_halo(padded, side, margin, links_ref, recv, tiles)
    conv(0)
    along = [go_along(0, over[0])]
    conv(1)
    along.append(go_along(1, over[1]))
    for copy in small:
        copy.wait()
    total = s_pack[...]
    for k in range(members - 1):
        total = total + sm_in[k]
    st_out[...] = total
    small = [
        remote(st_out.at[peer], st_in.at[k], st_sem, k, tile=peer) for k, peer in enumerate(peers)
    ]
    for part in range(2, parts):
        conv(part)
    back = send_back(0, along[0])
    for copy in small:
        copy.wait()
    total = st_out[tile]
    for k in range(tiles - 1):
        total = total + st_in[k]
    s_own[...] = total
    sout_ref[tile] = total
    small = [
        remote(s_own, sout_ref.at[tile], sg_sem, k, tile=peer) for k, peer in enumerate(peers)
    ]
    back = back + send_back(1, along[1])
    for copy in small + back:
        copy.wait()


def backward_all(links, grad, kern, cot, padded, grad_bin, grad_ch, big, side, members, tiles):
    _, _, spots, _, rows, width = big.shape
    taps = kern.shape[0]
    margin = taps // 2
    used = taps * taps + grad_bin.shape[1] // width + 5
    lines = 8 * (-(-used // (8 * tiles)))
    dma = lambda n: pltpu.SemaphoreType.DMA((2, max(n, 1)))
    return pl.pallas_call(
        functools.partial(backward_kernel, side, taps, members, tiles),
        in_specs=[smem_spec()] + [vmem_spec()] * 7,
        out_specs=[vmem_spec()] * 3,
        out_shape=[
            jax.ShapeDtypeStruct(cot.shape, BF16),
            jax.ShapeDtypeStruct((2, members, rows, width), BF16),
            jax.ShapeDtypeStruct((tiles, lines, width), F32),
        ],
        scratch_shapes=[pltpu.VMEM(padded.shape, F32)]
        + halo_scratch(side, margin, width)
        + [
            pltpu.VMEM((2, tiles, spots, rows, width), BF16),
            pltpu.VMEM((2, spots, tiles, rows, width), BF16),
            pltpu.VMEM((2, max(spots - 1, 1), tiles, rows, width), BF16),
            pltpu.VMEM((2, tiles, rows, width), BF16),
            pltpu.VMEM((2, tiles - 1, rows, width), BF16),
            pltpu.VMEM((2, rows, width), BF16),
            pltpu.VMEM((tiles, lines, width), F32),
            pltpu.VMEM((members - 1, tiles, lines, width), F32),
            pltpu.VMEM((tiles, lines, width), F32),
            pltpu.VMEM((tiles - 1, lines, width), F32),
            pltpu.VMEM((lines, width), F32),
            dma(2),
            dma(2 * (spots - 1)),
            dma(2 * (tiles - 1)),
            dma(2 * (members - 1)),
            dma(members - 1),
            dma(tiles - 1),
            dma(tiles - 1),
        ],
        compiler_params=remote_params(1),
        name="backward_all",
    )(links, grad, kern, cot, padded, grad_bin, grad_ch, big)


def body(
    state,
    cotangent,
    neighbors,
    kernel,
    conv_bias,
    norm_gain,
    norm_shift,
    w_in,
    bias_in,
    w_out,
    bias_out,
    layer_scale,
):
    side, width = state.shape[2], state.shape[4]
    cells = side * side
    center = state.reshape(cells, width)
    cot = cotangent.reshape(cells, width)
    hidden = w_in.shape[1]
    taps = kernel.shape[0]
    tiles = lax.axis_size("tile")
    members = lax.axis_size("member")
    mixed, padded = forward_conv(neighbors, center, kernel, conv_bias, side, taps, tiles)
    vectors = (norm_gain, norm_shift, bias_out, layer_scale)
    new_tile, grad_mixed, grad_w, grad_bin, grad_ch = pointwise(
        mixed, center, cot, w_in, w_out, bias_in, vectors
    )
    share = hidden // tiles
    rows = share // members
    big = grad_w.reshape(2, tiles, members // 2, 2, rows, width)
    state_grad, big, small = backward_all(
        neighbors, grad_mixed, kernel, cot, padded, grad_bin, grad_ch, big, side, members, tiles
    )
    factor = 1.0 / math.sqrt(members * tiles * cells)
    big = big.astype(F32) * factor
    win_share = big[0].reshape(share, width).T
    wout_share = big[1].reshape(share, width)
    small = small.reshape(-1, width) * factor
    first = taps * taps
    second = first + hidden // width
    return (
        new_tile.reshape(state.shape),
        state_grad.reshape(state.shape),
        win_share,
        wout_share,
        small[:first].reshape(taps, taps, width),
        small[first:second].reshape(hidden),
        small[second : second + 5],
    )


def solution(mesh):
    tiled = P("member", "tile", None, None, None)
    in_specs = (tiled, tiled) + (P(),) * 10
    out_specs = (tiled, tiled, P(None, "tile"), P("tile", None), P(), P(), P())
    return jax.shard_map(body, mesh=mesh, in_specs=in_specs, out_specs=out_specs, check_vma=False)
```

time: 149 us -> 92 us (0.62); the launches traced: 147 us -> 91.8 us
  Pallas kernels: 129 us -> 85.5 us
  local copies, waits for them, and re-layouts: 11.4 us -> 3.6 us
  other arithmetic: 6.12 us -> 1.99 us
    pallas_call x7 -> x2, Pallas kernels: 110 us -> 66.5 us  [the longest x1 42.5 us: backward_all(): pl.pallas_call(functools.partial(backward_kernel, side, taps, members, ti...]
    another operation x5 -> x0, local copies, waits for them, and re-layouts: 3.35 us -> none  [body(): vectors = jnp.stack([norm_gain, norm_shift, bias_out, layer_scale] * 2)]
    broadcast_in_dim x2 -> x0, local copies, waits for them, and re-layouts: 2.54 us -> none  [the longest x1 1.29 us: body(): bias_in[None]]
    reshape x1 -> x0, other arithmetic: 1.54 us -> none  [body(): packed.reshape(count, lines, width)]
    reshape x2 -> x0, local copies, waits for them, and re-layouts: 1.54 us -> none  [the longest x1 1.54 us: body(): flat_kernel = kernel.reshape(taps * taps, width)]
where the time goes in v2:
time: 92 us; the launch traced here: 91.8 us
  Pallas kernels  85.5 us (93%)
  local copies, waits for them, and re-layouts  3.6 us (4%)
  other arithmetic  1.99 us (2%)
    pallas_call x1, Pallas kernels, backward_all(): pl.pallas_call(functools.partial(backward_kernel, side, taps, members, ti...  42.5 us
    pallas_call x1, Pallas kernels, forward_conv(): pl.pallas_call(functools.partial(forward_kernel, side, taps, count), in_s...  24 us
    pallas_call x1, Pallas kernels, pointwise(): pl.pallas_call(functools.partial(mlp_kernel, chunk), grid=(cells // block...  19 us

profile of v2, /device:TPU:0, one launch (start us, length us, event | category | flops | bytes accessed | tf_op | source)
XLA Modules:
  0.0 91.8 jit_solution(9364861046241735234)
XLA Ops:
  0.6 24.0 %forward_conv.1 = (f32[1024,384]{1,0:T(8,128)}, f32[3,1824,128]{2,1,0:T(8,128)}) custom-call(s32[8,8]{1,0:T(8,128)} %links_ref.3, bf16[1024,384]{1,0:T(8,128)(2,1)} %bitcast.13, f32[7,7,384]{2,1,0:T(8,128)} %kern_ref.3, f32[384]{0:T(512)} %bias_ref.1), custom_call_target="tpu_custom_call" | custom-call | tf_op jit(solution)/shard_map/forward_conv/pallas_call | solution.py:255
  24.7 19.0 %pointwise.1 = (bf16[1024,384]{1,0:T(8,128)(2,1)}, f32[3,1024,128]{2,1,0:T(8,128)}, bf16[2,1536,384]{2,1,0:T(8,128)(2,1)}, f32[1,1536]{1,0:T(1,128)}, f32[8,384]{1,0:T(8,128)}) custom-call(f32[1024,384]{1,0:T(8,128)} %get-tuple-element.17.mixed_ref, bf16[1024,384]{1,0:T(8,128)(2,1)} %bitcast.14, bf16[1024,384]{1,0:T(8,128)(2,1)} %bitcast.11, ...), custom_call_target="tpu_custom_call" | custom-call | tf_op jit(solution)/shard_map/pointwise/pallas_call | solution.py:366
  43.6 42.5 %backward_all.1 = (bf16[1024,384]{1,0:T(8,128)(2,1)}, bf16[2,4,48,384]{3,2,1,0:T(8,128)(2,1)}, f32[8,8,384]{2,1,0:T(8,128)}) custom-call(s32[8,8]{1,0:T(8,128)} %links_ref.3, f32[3,1024,128]{2,1,0:T(8,128)} %get-tuple-element.19.grad_ref, f32[7,7,384]{2,1,0:T(8,128)} %kern_ref.3, bf16[1024,384]{1,0:T(8,128)(2,1)} %bitcast.12, ...), custom_call_target="tpu_custom_call" | custom-call | tf_op jit(solution)/shard_map/backward_all/pallas_call | solution.py:600
  86.2 0.0 copy-start
  86.2 1.0 %multiply_bitcast_fusion = f32[64,384]{1,0:T(8,128)S(1)} fusion(f32[8,8,384]{2,1,0:T(8,128)} %get-tuple-element.26), kind=kLoop, calls=%fused_computation.1 | loop fusion | flops 24576 | bytes 196608 | tf_op jit(solution)/shard_map/mul | solution.py:673
  87.2 0.6 reshape.44
  87.8 0.6 slice.24
  88.4 0.6 reshape.43
  89.0 1.0 %convert_multiply_fusion = f32[2,4,48,384]{3,2,1,0:T(8,128)S(1)} fusion(bf16[2,4,48,384]{3,2,1,0:T(8,128)(2,1)} %get-tuple-element.25), kind=kLoop, calls=%fused_computation | loop fusion | flops 294912 | bytes 884736 | tf_op jit(solution)/shard_map/mul | solution.py:670
  90.0 0.9 fusion
  90.9 0.0 copy-done
  90.9 0.9 copy.20
  (2 shorter events, 0.0 us)
Async XLA Ops:
  86.2 4.7 %copy-start = (bf16[1024,384]{1,0:T(8,128)(2,1)S(1)}, bf16[1024,384]{1,0:T(8,128)(2,1)}, u32[]{:S(2)}) copy-start(bf16[1024,384]{1,0:T(8,128)(2,1)} %get-tuple-element.24) | copy-start | bytes 2359300

commit v3 on v2

--- a/solution.py
+++ b/solution.py
@@ -124,13 +124,13 @@
                 padded[part, at, :] = line
 
 
-def convolve(padded, part, kern_ref, side, taps, flipped, emit, group=4):
+def convolve(padded, part, kern_ref, side, taps, flipped, emit, group=4, first=0, gap=1, steps=None):
     pitch = pitch_of(side)
     margin = taps // 2
     lanes = pl.ds(part * LANES, LANES)
 
     def step(index, carry):
-        base = index * group
+        base = (first + index * gap) * group
         total = [jnp.zeros((side, LANES), F32) for _ in range(group)]
         for col in range(taps):
             for row in range(group + taps - 1):
@@ -145,7 +145,32 @@
             emit(pl.multiple_of((base + out) * side, side), total[out])
         return carry
 
-    lax.fori_loop(0, side // group, step, 0)
+    lax.fori_loop(0, side // group if steps is None else steps, step, 0)
+
+
+def edge_columns(sides, part, kern_ref, side, taps, add, group=4):
+    margin = taps // 2
+    lanes = pl.ds(part * LANES, LANES)
+
+    def step(index, carry):
+        base = (1 + index) * group
+        for east in range(2):
+            total = [jnp.zeros((8, LANES), F32) for _ in range(group)]
+            for near in range(margin):
+                col = margin + 1 + near if east else near
+                shift = 1 + near if east else 8 - margin + near
+                for row in range(group + taps - 1):
+                    line = sides[east, part, pl.ds((base + row) * 16 + shift, 8), :]
+                    for out in range(group):
+                        up = row - out
+                        if 0 <= up < taps:
+                            total[out] = total[out] + kern_ref[up, pl.ds(col, 1), lanes] * line
+            for out in range(group):
+                start = (base + out) * side + (side - 8 if east else 0)
+                add(pl.multiple_of(start, 8), total[out])
+        return carry
+
+    lax.fori_loop(0, side // group - 2, step, 0)
 
 
 def kernel_grad(padded, part, grad_ref, side, taps, emit, group=4):
@@ -210,7 +235,7 @@
 
 
 def forward_kernel(
-    side, taps, count, links_ref, tile_ref, kern_ref, bias_ref, mixed_ref, padded, send, recv, sems
+    side, taps, count, links_ref, tile_ref, kern_ref, bias_ref, mixed_ref, padded, send, recv, sems, sides
 ):
     margin = taps // 2
     barrier = pltpu.get_barrier_semaphore()
@@ -227,17 +252,49 @@
         padded, side, margin, links_ref, send, recv, sems, count,
         lambda: pl.semaphore_wait(barrier, len(OFFSETS)),
     )
+    parts = padded.shape[0]
+    groups = side // 4
+    pitch = pitch_of(side)
+
+    def make_emit(part):
+        lanes = pl.ds(part * LANES, LANES)
+        bias = bias_ref[lanes].reshape(1, LANES)
+
+        def emit(start, value):
+            mixed_ref[pl.ds(start, side), lanes] = value + bias
+
+        return emit
+
+    for part in range(parts):
+        convolve(
+            padded, part, kern_ref, side, taps, False, make_emit(part), first=1, steps=groups - 2
+        )
     for copy in copies:
         copy.wait()
     take_halo(padded, side, margin, links_ref, recv, count)
-    for part in range(padded.shape[0]):
+    for part in range(parts):
         lanes = pl.ds(part * LANES, LANES)
-        bias = bias_ref[lanes].reshape(1, LANES)
-
-        def emit(start, value):
-            mixed_ref[pl.ds(start, side), lanes] = value + bias
-
-        convolve(padded, part, kern_ref, side, taps, False, emit)
+
+        def frame(row, carry):
+            at = pl.ds(pl.multiple_of(row * 16, 8), 8)
+            after = pl.ds(pl.multiple_of(row * 16 + 8, 8), 8)
+            start = row * pitch + LEAD
+            blank = jnp.zeros((8, LANES), F32)
+            sides[0, part, at, :] = padded[part, pl.ds(pl.multiple_of(start - 8, 8), 8), :]
+            sides[0, part, after, :] = blank
+            sides[1, part, at, :] = blank
+            sides[1, part, after, :] = padded[part, pl.ds(pl.multiple_of(start + side, 8), 8), :]
+            return carry
+
+        lax.fori_loop(0, side + 2 * margin, frame, 0)
+
+        def add(start, value):
+            mixed_ref[pl.ds(start, 8), lanes] += value
+
+        convolve(
+            padded, part, kern_ref, side, taps, False, make_emit(part), gap=groups - 1, steps=2
+        )
+        edge_columns(sides, part, kern_ref, side, taps, add)
 
 
 def halo_scratch(side, margin, width):
@@ -260,7 +317,8 @@
             jax.ShapeDtypeStruct((cells, width), F32),
             jax.ShapeDtypeStruct((width // LANES, spread_of(side, margin), LANES), F32),
         ],
-        scratch_shapes=halo_scratch(side, margin, width),
+        scratch_shapes=halo_scratch(side, margin, width)
+        + [pltpu.VMEM((2, width // LANES, (side + 2 * margin) * 16, LANES), F32)],
         compiler_params=remote_params(0),
         name="forward_conv",
     )(links, tile, kern, bias)
@@ -453,11 +511,7 @@
         at = pl.ds(pl.multiple_of(row * side, side), side)
         return grad_ref[part, at, :].astype(BF16).astype(F32)
 
-    place(padded, side, margin, center)
-    halo = swap_halo(
-        padded, side, margin, links_ref, send, recv, sems, tiles,
-        lambda: pl.semaphore_wait(barrier, members + tiles - 2),
-    )
+    pl.semaphore_wait(barrier, members + tiles - 2)
     pair = [
         remote(
             big_ref.at[kind, :, :, 1 - core], core_in.at[kind], core_sem, kind,
@@ -466,6 +520,10 @@
         for kind in range(2)
     ]
 
+    place(padded, side, margin, center)
+    halo = swap_halo(
+        padded, side, margin, links_ref, send, recv, sems, tiles, lambda: None
+    )
     lines = s_pack.shape[1]
     s_pack[...] = jnp.zeros_like(s_pack)
     width = s_pack.shape[2]
@@ -549,11 +607,8 @@
             for k, mate in enumerate(mates)
         ]
 
-    own_kernel(0)
-    over = [cross_over(0)]
-    own_kernel(1)
-    over.append(cross_over(1))
-    for part in range(2, parts):
+    over = [cross_over(0), cross_over(1)]
+    for part in range(parts):
         own_kernel(part)
     small = [remote(s_pack, sm_in.at[k], sm_sem, k, member=mate) for k, mate in enumerate(mates)]
     for copy in halo:
@@ -633,6 +688,41 @@
     )(links, grad, kern, cot, padded, grad_bin, grad_ch, big)
 
 
+def finish_kernel(taps, factor, big_ref, small_ref, win_ref, wout_ref, kern_ref, bin_ref, ch_ref, wide):
+    _, members, rows, width = big_ref.shape
+    lines = small_ref.shape[1]
+    for m in range(members):
+        wide[pl.ds(m * rows, rows), :] = big_ref[0, m].astype(F32) * factor
+        wout_ref[pl.ds(m * rows, rows), :] = big_ref[1, m].astype(F32) * factor
+    win_ref[...] = wide[...].T
+
+    def line(at):
+        return small_ref[at // lines, pl.ds(at % lines, 1), :] * factor
+
+    for at in range(taps * taps):
+        kern_ref[at // taps, pl.ds(at % taps, 1), :] = line(at)
+    first = taps * taps
+    extra = bin_ref.shape[0] // width
+    for at in range(extra):
+        bin_ref[pl.ds(at * width, width)] = line(first + at).reshape(width)
+    for at in range(5):
+        ch_ref[pl.ds(at, 1), :] = line(first + extra + at)
+
+
+def finish(big, small, share, taps, hidden, factor):
+    width = big.shape[3]
+    shapes = [(width, share), (share, width), (taps, taps, width), (hidden,), (5, width)]
+    return pl.pallas_call(
+        functools.partial(finish_kernel, taps, factor),
+        in_specs=[vmem_spec()] * 2,
+        out_specs=[vmem_spec()] * 5,
+        out_shape=[jax.ShapeDtypeStruct(shape, F32) for shape in shapes],
+        scratch_shapes=[pltpu.VMEM((share, width), F32)],
+        compiler_params=local_params(),
+        name="finish",
+    )(big, small)
+
+
 def body(
     state,
     cotangent,
@@ -667,20 +757,11 @@
         neighbors, grad_mixed, kernel, cot, padded, grad_bin, grad_ch, big, side, members, tiles
     )
     factor = 1.0 / math.sqrt(members * tiles * cells)
-    big = big.astype(F32) * factor
-    win_share = big[0].reshape(share, width).T
-    wout_share = big[1].reshape(share, width)
-    small = small.reshape(-1, width) * factor
-    first = taps * taps
-    second = first + hidden // width
+    shares = finish(big, small, share, taps, hidden, factor)
     return (
         new_tile.reshape(state.shape),
         state_grad.reshape(state.shape),
-        win_share,
-        wout_share,
-        small[:first].reshape(taps, taps, width),
-        small[first:second].reshape(hidden),
-        small[second : second + 5],
+        *shares,
     )
 
 

time: 92 us -> 90.4 us (0.983)
  other arithmetic: 1.99 us -> 0 us
  Pallas kernels: 85.5 us -> 86.8 us
    pallas_call x1, Pallas kernels: 24 us -> 21.6 us  [forward_conv(): pl.pallas_call(functools.partial(forward_kernel, side, taps, count), in_s...]
    pallas_call x0 -> x1, Pallas kernels: none -> 2.05 us  [finish(): pl.pallas_call(functools.partial(finish_kernel, taps, factor), in_specs=[...]
    mul x2 -> x0, other arithmetic: 1.99 us -> none  [the longest x1 1.01 us: body(): big = big.astype(F32) * factor]
    unnamed x3 -> x4, local copies, waits for them, and re-layouts: 0.88 us -> 2.74 us
    pallas_call x1, Pallas kernels: 42.5 us -> 44.2 us  [backward_all(): pl.pallas_call(functools.partial(backward_kernel, side, taps, members, ti...]
    slice x4 -> x0, local copies, waits for them, and re-layouts: 1.46 us -> none  [the longest x1 0.85 us: body(): wout_share = big[1].reshape(share, width)]
    reshape x2 -> x0, local copies, waits for them, and re-layouts: 1.25 us -> none  [the longest x1 0.65 us: body(): small[:first].reshape(taps, taps, width)]
where the time goes in v3:
time: 90.4 us; the launch traced here: 90.2 us
  Pallas kernels  86.8 us (96%)
  local copies, waits for them, and re-layouts  2.74 us (3%)
    pallas_call x1, Pallas kernels, backward_all(): pl.pallas_call(functools.partial(backward_kernel, side, taps, members, ti...  44.2 us
    pallas_call x1, Pallas kernels, forward_conv(): pl.pallas_call(functools.partial(forward_kernel, side, taps, count), in_s...  21.6 us
    pallas_call x1, Pallas kernels, pointwise(): pl.pallas_call(functools.partial(mlp_kernel, chunk), grid=(cells // block...  19 us
    unnamed x4, local copies, waits for them, and re-layouts  2.74 us
    pallas_call x1, Pallas kernels, finish(): pl.pallas_call(functools.partial(finish_kernel, taps, factor), in_specs=[...  2.05 us

profile of v3, /device:TPU:0, one launch (start us, length us, event | category | flops | bytes accessed | tf_op | source)
XLA Modules:
  0.0 90.2 jit_solution(2303085900187900397)
XLA Ops:
  0.6 21.6 %forward_conv.1 = (f32[1024,384]{1,0:T(8,128)}, f32[3,1824,128]{2,1,0:T(8,128)}) custom-call(s32[8,8]{1,0:T(8,128)} %links_ref.3, bf16[1024,384]{1,0:T(8,128)(2,1)} %bitcast.7, f32[7,7,384]{2,1,0:T(8,128)} %kern_ref.3, f32[384]{0:T(512)} %bias_ref.1), custom_call_target="tpu_custom_call" | custom-call | tf_op jit(solution)/shard_map/forward_conv/pallas_call | solution.py:312
  22.3 19.0 %pointwise.1 = (bf16[1024,384]{1,0:T(8,128)(2,1)}, f32[3,1024,128]{2,1,0:T(8,128)}, bf16[2,1536,384]{2,1,0:T(8,128)(2,1)}, f32[1,1536]{1,0:T(1,128)}, f32[8,384]{1,0:T(8,128)}) custom-call(f32[1024,384]{1,0:T(8,128)} %get-tuple-element.22.mixed_ref, bf16[1024,384]{1,0:T(8,128)(2,1)} %bitcast.8, bf16[1024,384]{1,0:T(8,128)(2,1)} %bitcast.5, ...), custom_call_target="tpu_custom_call" | custom-call | tf_op jit(solution)/shard_map/pointwise/pallas_call | solution.py:424
  41.2 44.2 %backward_all.1 = (bf16[1024,384]{1,0:T(8,128)(2,1)}, bf16[2,4,48,384]{3,2,1,0:T(8,128)(2,1)}, f32[8,8,384]{2,1,0:T(8,128)}) custom-call(s32[8,8]{1,0:T(8,128)} %links_ref.3, f32[3,1024,128]{2,1,0:T(8,128)} %get-tuple-element.24.grad_ref, f32[7,7,384]{2,1,0:T(8,128)} %kern_ref.3, bf16[1024,384]{1,0:T(8,128)(2,1)} %bitcast.6, ...), custom_call_target="tpu_custom_call" | custom-call | tf_op jit(solution)/shard_map/backward_all/pallas_call | solution.py:655
  85.4 0.0 copy-start
  85.4 2.1 %finish.1 = (f32[384,192]{1,0:T(8,128)}, f32[192,384]{1,0:T(8,128)}, f32[7,7,384]{2,1,0:T(8,128)}, f32[1536]{0:T(1024)}, f32[5,384]{1,0:T(8,128)}) custom-call(bf16[2,4,48,384]{3,2,1,0:T(8,128)(2,1)} %get-tuple-element.30.big_ref, f32[8,8,384]{2,1,0:T(8,128)} %get-tuple-element.31.small_ref), custom_call_target="tpu_custom_call" | custom-call | tf_op jit(solution)/shard_map/finish/pallas_call | solution.py:715
  87.5 1.9 %copy.19 = f32[384,192]{0,1:T(8,128)} copy(f32[384,192]{1,0:T(8,128)} %get-tuple-element.39) | data formatting | bytes 589824
  89.3 0.0 copy-done
  89.3 0.9 copy.21
Async XLA Ops:
  85.4 3.9 %copy-start = (bf16[1024,384]{1,0:T(8,128)(2,1)S(1)}, bf16[1024,384]{1,0:T(8,128)(2,1)}, u32[]{:S(2)}) copy-start(bf16[1024,384]{1,0:T(8,128)(2,1)} %get-tuple-element.29) | copy-start | bytes 2359300

commit v4 on v3

--- a/solution.py
+++ b/solution.py
@@ -416,7 +416,7 @@
         gw_ref[...] = acc_ref[...].astype(BF16)
 
 
-def pointwise(mixed, state, cot, w_in, w_out, bias_in, vectors, block=256, chunk=512):
+def pointwise(mixed, state, cot, w_in, w_out, bias_in, vectors, block=512, chunk=768):
     cells, width = mixed.shape
     hidden = w_in.shape[1]
     cell = lambda r: (r, 0)
@@ -607,8 +607,11 @@
             for k, mate in enumerate(mates)
         ]
 
-    over = [cross_over(0), cross_over(1)]
-    for part in range(parts):
+    own_kernel(0)
+    over = [cross_over(0)]
+    own_kernel(1)
+    over.append(cross_over(1))
+    for part in range(2, parts):
         own_kernel(part)
     small = [remote(s_pack, sm_in.at[k], sm_sem, k, member=mate) for k, mate in enumerate(mates)]
     for copy in halo:
@@ -688,13 +691,12 @@
     )(links, grad, kern, cot, padded, grad_bin, grad_ch, big)
 
 
-def finish_kernel(taps, factor, big_ref, small_ref, win_ref, wout_ref, kern_ref, bin_ref, ch_ref, wide):
+def finish_kernel(taps, factor, big_ref, small_ref, win_ref, wout_ref, kern_ref, bin_ref, ch_ref):
     _, members, rows, width = big_ref.shape
     lines = small_ref.shape[1]
     for m in range(members):
-        wide[pl.ds(m * rows, rows), :] = big_ref[0, m].astype(F32) * factor
+        win_ref[pl.ds(m * rows, rows), :] = big_ref[0, m].astype(F32) * factor
         wout_ref[pl.ds(m * rows, rows), :] = big_ref[1, m].astype(F32) * factor
-    win_ref[...] = wide[...].T
 
     def line(at):
         return small_ref[at // lines, pl.ds(at % lines, 1), :] * factor
@@ -711,13 +713,12 @@
 
 def finish(big, small, share, taps, hidden, factor):
     width = big.shape[3]
-    shapes = [(width, share), (share, width), (taps, taps, width), (hidden,), (5, width)]
+    shapes = [(share, width), (share, width), (taps, taps, width), (hidden,), (5, width)]
     return pl.pallas_call(
         functools.partial(finish_kernel, taps, factor),
         in_specs=[vmem_spec()] * 2,
         out_specs=[vmem_spec()] * 5,
         out_shape=[jax.ShapeDtypeStruct(shape, F32) for shape in shapes],
-        scratch_shapes=[pltpu.VMEM((share, width), F32)],
         compiler_params=local_params(),
         name="finish",
     )(big, small)
@@ -757,10 +758,11 @@
         neighbors, grad_mixed, kernel, cot, padded, grad_bin, grad_ch, big, side, members, tiles
     )
     factor = 1.0 / math.sqrt(members * tiles * cells)
-    shares = finish(big, small, share, taps, hidden, factor)
+    win_share, *shares = finish(big, small, share, taps, hidden, factor)
     return (
         new_tile.reshape(state.shape),
         state_grad.reshape(state.shape),
+        win_share.T,
         *shares,
     )
 

time: 90.4 us -> 87.2 us (0.965)
  Pallas kernels: 86.8 us -> 84.3 us
    pallas_call x1, Pallas kernels: 19 us -> 17.3 us  [pointwise(): pl.pallas_call(functools.partial(mlp_kernel, chunk), grid=(cells // block...]
    unnamed x4 -> x1, local copies, waits for them, and re-layouts: 2.74 us -> 2.09 us
where the time goes in v4:
time: 87.2 us; the launch traced here: 87 us
  Pallas kernels  84.3 us (97%)
  local copies, waits for them, and re-layouts  2.09 us (2%)
    pallas_call x1, Pallas kernels, backward_all(): pl.pallas_call(functools.partial(backward_kernel, side, taps, members, ti...  43.5 us
    pallas_call x1, Pallas kernels, forward_conv(): pl.pallas_call(functools.partial(forward_kernel, side, taps, count), in_s...  21.6 us
    pallas_call x1, Pallas kernels, pointwise(): pl.pallas_call(functools.partial(mlp_kernel, chunk), grid=(cells // block...  17.3 us
    unnamed x1, local copies, waits for them, and re-layouts  2.09 us
    pallas_call x1, Pallas kernels, finish(): pl.pallas_call(functools.partial(finish_kernel, taps, factor), in_specs=[...  1.86 us

profile of v4, /device:TPU:0, one launch (start us, length us, event | category | flops | bytes accessed | tf_op | source)
XLA Modules:
  0.0 87.0 jit_solution(12045818147257662334)
XLA Ops:
  0.6 21.6 %forward_conv.1 = (f32[1024,384]{1,0:T(8,128)}, f32[3,1824,128]{2,1,0:T(8,128)}) custom-call(s32[8,8]{1,0:T(8,128)} %links_ref.3, bf16[1024,384]{1,0:T(8,128)(2,1)} %bitcast.8, f32[7,7,384]{2,1,0:T(8,128)} %kern_ref.3, f32[384]{0:T(512)} %bias_ref.1), custom_call_target="tpu_custom_call" | custom-call | tf_op jit(solution)/shard_map/forward_conv/pallas_call | solution.py:312
  22.3 17.3 %pointwise.1 = (bf16[1024,384]{1,0:T(8,128)(2,1)}, f32[3,1024,128]{2,1,0:T(8,128)}, bf16[2,1536,384]{2,1,0:T(8,128)(2,1)}, f32[1,1536]{1,0:T(1,128)}, f32[8,384]{1,0:T(8,128)}) custom-call(f32[1024,384]{1,0:T(8,128)} %get-tuple-element.22.mixed_ref, bf16[1024,384]{1,0:T(8,128)(2,1)} %bitcast.9, bf16[1024,384]{1,0:T(8,128)(2,1)} %bitcast.6, ...), custom_call_target="tpu_custom_call" | custom-call | tf_op jit(solution)/shard_map/pointwise/pallas_call | solution.py:424
  39.6 43.5 %backward_all.1 = (bf16[1024,384]{1,0:T(8,128)(2,1)}, bf16[2,4,48,384]{3,2,1,0:T(8,128)(2,1)}, f32[8,8,384]{2,1,0:T(8,128)}) custom-call(s32[8,8]{1,0:T(8,128)} %links_ref.3, f32[3,1024,128]{2,1,0:T(8,128)} %get-tuple-element.24.grad_ref, f32[7,7,384]{2,1,0:T(8,128)} %kern_ref.3, bf16[1024,384]{1,0:T(8,128)(2,1)} %bitcast.7, ...), custom_call_target="tpu_custom_call" | custom-call | tf_op jit(solution)/shard_map/backward_all/pallas_call | solution.py:658
  83.1 1.9 %finish.1 = (f32[192,384]{1,0:T(8,128)}, f32[192,384]{1,0:T(8,128)}, f32[7,7,384]{2,1,0:T(8,128)}, f32[1536]{0:T(1024)}, f32[5,384]{1,0:T(8,128)}) custom-call(bf16[2,4,48,384]{3,2,1,0:T(8,128)(2,1)} %get-tuple-element.30.big_ref, f32[8,8,384]{2,1,0:T(8,128)} %get-tuple-element.31.small_ref), custom_call_target="tpu_custom_call" | custom-call | tf_op jit(solution)/shard_map/finish/pallas_call | solution.py:717
  84.9 2.1 %copy.20 = bf16[1,1,32,32,384]{4,3,2,1,0:T(8,128)(2,1)} copy(bf16[1,1,32,32,384]{4,3,2,1,0:T(8,128)(2,1)} %bitcast.11) | data formatting | bytes 1572864
